TPU v7x, 32 devices: a whole 2x2x4 slice. The times are simulated.
32 devices in a mesh: basin: 2 (over x), recv: 8 (over z, y), src: 2 (over core).
Axes of the slice: x: 2, y: 2, z: 4, core: 2. Of those that a mesh axis runs over, the one named last changes fastest.
Arguments:
- positions: float32 [3, 4096], P(None, ('basin', 'recv', 'src')), parts along dimension 1, may hold values from -1.1 to 1.1, as said below
- normals: float32 [3, 4096], P(None, ('basin', 'recv', 'src')), parts along dimension 1, may hold values from -1 to 1, as said below
- area: float32 [4096], P(('basin', 'recv', 'src')), parts along dimension 0, may hold values from 0.0009765625 to 0.0078125
- albedo: float32 [4096], P(('basin', 'recv', 'src')), parts along dimension 0, may hold values from 0.1 to 0.6
- conductivity: float32 [4096], P(('basin', 'recv', 'src')), parts along dimension 0, may hold values from 0.05 to 0.4
- soil: float32 [32, 4096], P(None, ('basin', 'recv', 'src')), parts along dimension 1, may hold values from 0.5 to 1.2
- sun_tan: float32 [16], replicated, may hold values from 0.05 to 2
- samples: int32 [32, 32], P(('basin', 'recv', 'src')), parts along dimension 0, may hold values from 1 to 2047
- occupancy: int32 [32, 16], P('basin'), parts along dimension 0, may hold values 0 or 1
Outputs:
- soil_final: float32 [32, 4096], P(None, ('basin', 'recv', 'src')), parts along dimension 1
- bounce: float32 [16, 4096], P(None, ('basin', 'recv', 'src')), parts along dimension 1
There are 2 independent parts, one for each index of `basin`. A program takes and returns all parts, laid end to end along the dimension named above; an argument that names none is the same for every part. Nothing has to cross between parts.
Inputs may be any that keep to these rules, and one draw needn't show every extreme that they name: `positions`: facets lie on a bowl below z = 0. `normals`: each column has unit length.
All inputs are finite; a program needn't handle non-finite values.
Results may differ from a plain program's by a relative error of at most 0.0003.
Values may be sent and summed in bfloat16 or wider, within the bound.
No kernel may reach another device: no remote copies, remote signals or barrier semaphores. Data moves between devices by JAX's collectives and lax.ppermute only.
A program may use at most 64 MiB of HBM per device.

v0:
```python
import math

import jax
import jax.numpy as jnp
from jax import lax
from jax.sharding import PartitionSpec as P

solar_flux = 2.0
emissivity = 0.9
surface_gain = 0.1
shade_width = 0.1
reach_offset = 0.05


def partner(value, axis, apart):
    mask = 2**apart
    pairs = [(source, source ^ mask) for source in range(lax.axis_size(axis))]
    return lax.ppermute(value, axis, pairs)


def fourth(value):
    square = value * value
    return square * square


def rotate(values, shift):
    count = values.shape[0]
    doubled = jnp.concatenate([values, values], 0)
    return lax.dynamic_slice_in_dim(doubled, shift, count, 0)


def profile_max(coords, offsets):
    px, py, pz = (coords[0], coords[1], coords[2])
    count = px.shape[0]

    def sweep(best, shift):
        delta_x = rotate(px, shift) - px
        delta_y = rotate(py, shift) - py
        reach = jnp.sqrt(delta_x * delta_x + delta_y * delta_y) + reach_offset
        slope = (rotate(pz, shift) - pz) / reach
        return (jnp.maximum(best, slope), None)

    start = jnp.full((count,), -1e30, jnp.float32)
    best, unused = lax.scan(sweep, start, offsets)
    return best


def horizons(coords, samples):
    return lax.map(lambda offsets: profile_max(coords, offsets), samples)


def sunlight(facing, sun_tan, horizon):
    count = sun_tan.shape[0]
    angle = 2.0 * math.pi * jnp.arange(count, dtype=jnp.float32) / count
    elevation = jnp.arctan(sun_tan)
    sun_x = jnp.cos(elevation) * jnp.cos(angle)
    sun_y = jnp.cos(elevation) * jnp.sin(angle)
    sun_z = jnp.sin(elevation)
    incidence = (
        sun_x[:, None] * facing[0][None, :]
        + sun_y[:, None] * facing[1][None, :]
        + sun_z[:, None] * facing[2][None, :]
    )
    shade = jax.nn.sigmoid((sun_tan[:, None] - horizon) / shade_width)
    return solar_flux * jnp.maximum(incidence, 0.0) * shade


def conduct(soil, direct, bounce, albedo, conductivity):

    def advance(temps, inputs):
        light, scattered = inputs
        grad = temps[1:] - temps[:-1]
        edge = jnp.zeros((1, temps.shape[1]), jnp.float32)
        change = jnp.concatenate([grad, edge], 0) - jnp.concatenate([edge, grad], 0)
        temps = temps + conductivity[None, :] * change
        absorbed = (1.0 - albedo) * (light + scattered)
        top = temps[0] + surface_gain * (absorbed - emissivity * fourth(temps[0]))
        return (jnp.concatenate([top[None, :], temps[1:]], 0), None)

    final, unused = lax.scan(advance, soil, (direct, bounce))
    return final


def view_tile(src_pos, src_nrm, src_area, src_ids, rec_pos, rec_nrm, mask_rows, width):
    onehot = (src_ids[:, None] == jnp.arange(mask_rows.shape[1], dtype=jnp.int32)[None, :]).astype(
        jnp.float32
    )
    weight = jnp.dot(
        onehot, mask_rows.T, preferred_element_type=jnp.float32, precision=lax.Precision.HIGHEST
    )
    weight = jnp.repeat(weight, width, axis=1)
    delta_x = src_pos[0][:, None] - rec_pos[0][None, :]
    delta_y = src_pos[1][:, None] - rec_pos[1][None, :]
    delta_z = src_pos[2][:, None] - rec_pos[2][None, :]
    facing = jnp.maximum(
        rec_nrm[0][None, :] * delta_x
        + rec_nrm[1][None, :] * delta_y
        + rec_nrm[2][None, :] * delta_z,
        0.0,
    )
    toward = jnp.maximum(
        -(
            src_nrm[0][:, None] * delta_x
            + src_nrm[1][:, None] * delta_y
            + src_nrm[2][:, None] * delta_z
        ),
        0.0,
    )
    spread = delta_x * delta_x + delta_y * delta_y + delta_z * delta_z + src_area[:, None]
    return (facing * toward * src_area[:, None] * weight / (math.pi * spread * spread)).astype(
        jnp.bfloat16
    )


def make_fold(src_pos, src_nrm, src_area, block_of, rec_pos, rec_nrm, mask_rows, width):

    def add_tile(carry, segment, begin, count):
        ids = block_of(begin + jnp.arange(count, dtype=jnp.int32))
        pos = lax.dynamic_slice_in_dim(src_pos, begin, count, 1)
        nrm = lax.dynamic_slice_in_dim(src_nrm, begin, count, 1)
        sizes = lax.dynamic_slice_in_dim(src_area, begin, count, 0)
        view = view_tile(pos, nrm, sizes, ids, rec_pos, rec_nrm, mask_rows, width)
        return carry + jnp.dot(segment, view, preferred_element_type=jnp.float32)

    def fold(carry, piece, start):
        count = piece.shape[1]

        def step_once(total, number):
            offset = number * width
            segment = lax.dynamic_slice_in_dim(piece, offset, width, 1)
            return (add_tile(total, segment, offset, width), None)

        total, unused = lax.scan(step_once, carry, jnp.arange(count // width, dtype=jnp.int32))
        return total

    return fold


def body(positions, normals, area, albedo, conductivity, soil, sun_tan, samples, occupancy):
    width = positions.shape[1]
    n_recv = lax.axis_size("recv")
    n_src = lax.axis_size("src")
    recv_index = lax.axis_index("recv")
    src_index = lax.axis_index("src")
    all_pos, all_nrm, all_area = (
        lax.all_gather(positions, ("recv", "src"), axis=1, tiled=True),
        lax.all_gather(normals, ("recv", "src"), axis=1, tiled=True),
        lax.all_gather(area, ("recv", "src"), axis=0, tiled=True),
    )
    horizon = horizons(all_pos, samples)
    facet_horizon = lax.all_to_all(
        horizon.astype(jnp.bfloat16), ("recv", "src"), split_axis=1, concat_axis=0, tiled=True
    ).astype(horizon.dtype)
    direct = sunlight(normals, sun_tan, facet_horizon)
    radiance = (albedo[None, :] * direct + emissivity * fourth(soil[0])[None, :]).astype(
        jnp.bfloat16
    )
    epochs = radiance.shape[0]
    table = occupancy.astype(jnp.float32)
    low_bits = recv_index % 4
    high_bits = recv_index // 4
    share = 4 * n_src
    rec_pos = lax.dynamic_slice_in_dim(all_pos, high_bits * share * width, share * width, 1)
    rec_nrm = lax.dynamic_slice_in_dim(all_nrm, high_bits * share * width, share * width, 1)
    mask_rows = lax.dynamic_slice_in_dim(table, high_bits * share, share, 0)
    column = low_bits * n_src + src_index

    def pick_class(values):
        lead = values.shape[:-1]
        arranged = values.reshape(lead + (n_recv // 4, share * width))
        chosen = lax.dynamic_slice_in_dim(arranged, column * width, width, len(lead) + 1)
        return chosen.reshape(lead + (n_recv // 4 * width,))

    def block_class(index):
        return index // width * share + column

    fold = make_fold(
        pick_class(all_pos),
        pick_class(all_nrm),
        pick_class(all_area),
        block_class,
        rec_pos,
        rec_nrm,
        mask_rows,
        width,
    )
    gathered = radiance
    for bit in range(2, n_recv.bit_length() - 1):
        other = partner(gathered, "recv", bit)
        upper = recv_index // (1 << bit) % 2 == 1
        gathered = jnp.where(
            upper, jnp.concatenate([other, gathered], 1), jnp.concatenate([gathered, other], 1)
        )
    start_sum = jnp.zeros((epochs, share * width), jnp.float32)
    partial_flux = fold(start_sum, gathered, jnp.int32(0))
    paired = lax.psum_scatter(
        partial_flux.reshape(epochs, 4, n_src, width), "src", scatter_dimension=2, tiled=True
    )
    paired = paired.reshape(epochs, 4, width)
    for bit in (1, 0):
        half = paired.shape[1] // 2
        lower = paired[:, :half]
        higher = paired[:, half:]
        upper = recv_index // (1 << bit) % 2 == 1
        keep = jnp.where(upper, higher, lower)
        outgoing = jnp.where(upper, lower, higher)
        paired = keep + partner(outgoing, "recv", bit)
    bounce = paired.reshape(epochs, width)
    final = conduct(soil, direct, bounce, albedo, conductivity)
    return (final, bounce)


def solution(mesh):
    in_specs = (
        P(None, ("basin", "recv", "src")),
        P(None, ("basin", "recv", "src")),
        P(("basin", "recv", "src")),
        P(("basin", "recv", "src")),
        P(("basin", "recv", "src")),
        P(None, ("basin", "recv", "src")),
        P(),
        P(("basin", "recv", "src"), None),
        P("basin", None),
    )
    out_specs = (P(None, ("basin", "recv", "src")), P(None, ("basin", "recv", "src")))
    return jax.shard_map(body, mesh=mesh, in_specs=in_specs, out_specs=out_specs, check_vma=False)
```

profile of v0, /device:TPU:0, one launch (start us, length us, event | category | flops | bytes accessed | tf_op | source)
XLA Modules:
  0.0 205.7 jit_solution(17961653555139462512)
XLA Ops:
  7.2 0.7 copy.50
  7.9 0.7 copy-done.6
  8.6 23.2 %all_gather.9 = f32[3,2048]{1,0:T(4,128)S(1)} all-gather(f32[3,128]{1,0:T(4,128)S(1)} %copy-done.6), channel_id=1, replica_groups=mesh['basin'=2,'recv'=8,'src'=2] {'recv','src'}, dimensions={1}, use_global_device_ids=true | all-gather | bytes 26112 | tf_op jit(solution)/shard_map/all_gather | solution.py:146
  32.5 91.5 %while.43 = (s32[]{:T(128)}, bf16[2048]{0:T(1024)(128)(2,1)S(1)}, s32[32]{0:T(128)S(1)}, f32[4096]{0:T(1024)S(1)}, f32[2048]{0:T(1024)S(1)}, /*index=5*/f32[4096...) while((s32[]{:T(128)}, bf16[2048]{0:T(1024)(128)(2,1)S(1)}, ...), condition=%wide.region_1.2_spmd.clone, body=%wide.region_0.1_spmd.clone.sunk | while | flops 24582 | bytes 57529 | solution.py:44
  35.3 0.7 dynamic_slice.136
  38.2 0.7 dynamic_slice.136
  41.0 0.7 dynamic_slice.136
  43.9 0.7 dynamic_slice.136
  46.7 0.7 dynamic_slice.136
  49.6 0.7 dynamic_slice.136
  124.5 3.5 %all-to-all-start = ((bf16[1,16,128]{2,0,1:T(2,128)(2,1)}), bf16[1,16,128]{2,0,1:T(2,128)(2,1)S(1)}, u32[]{:S(2)}, u32[]{:S(2)}) async-start(bf16[1,16,128]{2,0,1:T(2,128)(2,1)} %copy.16), calls=%async_computation | async-start | bytes 16384 | tf_op jit(solution)/shard_map/all_to_all | solution.py:151
  128.7 21.7 %all_gather.10 = f32[3,2048]{1,0:T(4,128)S(1)} all-gather(f32[3,128]{1,0:T(4,128)S(1)} %copy-done.5), channel_id=1, replica_groups=mesh['basin'=2,'recv'=8,'src'=2] {'recv','src'}, dimensions={1}, use_global_device_ids=true | all-gather | bytes 26112 | tf_op jit(solution)/shard_map/all_gather | solution.py:147
  152.0 17.4 %all-gather = f32[16,1,128]{2,1,0:T(1,128)S(1)} all-gather(f32[1,1,128]{2,1,0:T(1,128)S(1)} %bitcast.108), channel_id=1, replica_groups=mesh['basin'=2,'recv'=8,'src'=2] {'recv','src'}, dimensions={0}, use_global_device_ids=true | all-gather | bytes 8704 | tf_op jit(solution)/shard_map/all_gather | solution.py:148
  171.5 4.4 %collective-permute-done = bf16[16,128]{1,0:T(8,128)(2,1)S(1)} collective-permute-done((bf16[16,128]{1,0:T(8,128)(2,1)S(1)}, bf16[16,128]{1,0:T(8,128)(2,1)S(1)}, u32[]{:S(2)}, u32[]{:S(2)}) %collective-permute-start) | collective-permute-done | bytes 4128 | tf_op jit(solution)/shard_map/ppermute | solution.py:18
  175.9 5.1 %while.44 = (s32[]{:T(128)}, f32[16,1024]{1,0:T(8,128)S(1)}, s32[2]{0:T(128)S(1)}, bf16[16,256]{1,0:T(8,128)(2,1)S(1)}, f32[3,1024]{1,0:T(4,128)S(1)}, /*index=5...) while((s32[]{:T(128)}, f32[16,1024]{1,0:T(8,128)S(1)}, ...), condition=%wide.region_3.4_spmd.clone, body=%wide.region_2.3_spmd.clone.sunk | while | flops 8229127 | bytes 1284333 | solution.py:133
  177.6 0.8 convolution_add_fusion.2
  180.2 0.8 convolution_add_fusion.2
  181.7 6.1 %reduce-scatter.2.cloned.1.call-done = f32[16,4,1,128]{3,0,1,2:T(8,128)} async-done(((f32[16,4,2,128]{3,0,1,2:T(8,128)}), f32[16,4,1,128]{3,0,1,2:T(8,128)}) %reduce-scatter.2.cloned.1.call-update) | async-done | bytes 32784 | tf_op jit(solution)/shard_map/reduce_scatter | solution.py:196
  187.8 0.8 slice_select_fusion
  188.6 1.7 collective-permute-start.1
  190.3 2.1 %collective-permute-done.1 = f32[16,2,128]{2,0,1:T(8,128)S(1)} collective-permute-done((f32[16,2,128]{2,0,1:T(8,128)S(1)}, f32[16,2,128]{2,0,1:T(8,128)S(1)}, u32[]{:S(2)}, u32[]{:S(2)}) %collective-permute-start.1) | collective-permute-done | bytes 16416 | tf_op jit(solution)/shard_map/ppermute | solution.py:18
  192.4 1.7 collective-permute-start.2
  194.1 2.0 collective-permute-done.2
  196.7 1.5 while.42
  (212 shorter events, 30.9 us)
Async XLA Ops:
  7.9 0.7 copy-start.6
  31.8 0.7 copy-start.10
  124.5 46.0 %all-to-all-start = ((bf16[1,16,128]{2,0,1:T(2,128)(2,1)}), bf16[1,16,128]{2,0,1:T(2,128)(2,1)S(1)}, u32[]{:S(2)}, u32[]{:S(2)}) async-start(bf16[1,16,128]{2,0,1:T(2,128)(2,1)} %copy.16), calls=%async_computation | async-start | bytes 16384 | tf_op jit(solution)/shard_map/all_to_all | solution.py:151
  128.0 59.8 %reduce-scatter.2.cloned.1.call-start = ((), (), s32[]{:S(2)}) async-start(), calls=%async_computation.2 | async-start | bytes 98304 | tf_op jit(solution)/shard_map/reduce_scatter | solution.py:196
  128.1 0.7 copy-start.5
  150.5 0.7 copy-start.8
  150.5 0.7 copy-start.7
  151.3 0.7 copy-start.9
  170.6 0.7 copy-start.2
  171.3 4.6 %collective-permute-start = (bf16[16,128]{1,0:T(8,128)(2,1)S(1)}, bf16[16,128]{1,0:T(8,128)(2,1)S(1)}, u32[]{:S(2)}, u32[]{:S(2)}) collective-permute-start(bf16[16,128]{1,0:T(8,128)(2,1)S(1)} %get-tuple-element.374), channel_id=1, source_target_pairs={{0,8},{2,10},{4,12},{6,14},{8,0},{10,2},{12,4},{14,6},{1,9},{3,11}... | collective-permute-start | bytes 12296 | tf_op jit(solution)/shard_map/ppermute | solution.py:18
  187.8 4.5 %copy-start.1 = (f32[16,4,1,128]{3,0,1,2:T(8,128)S(1)}, f32[16,4,1,128]{3,0,1,2:T(8,128)}, u32[]{:S(2)}) copy-start(f32[16,4,1,128]{3,0,1,2:T(8,128)} %reduce-scatter.2.cloned.1.call-done) | copy-start | bytes 98308
  188.6 3.7 %collective-permute-start.1 = (f32[16,2,128]{2,0,1:T(8,128)S(1)}, f32[16,2,128]{2,0,1:T(8,128)S(1)}, u32[]{:S(2)}, u32[]{:S(2)}) collective-permute-start(f32[16,2,128]{2,0,1:T(8,128)S(1)} %slice_select_fusion), channel_id=1, source_target_pairs={{0,4},{2,6},{4,0},{6,2},{8,12},{10,14},{12,8},{14,10},{1,5},{3,7},... | collective-permute-start | bytes 49160 | tf_op jit(solution)/shard_map/ppermute | solution.py:18
  192.4 3.7 %collective-permute-start.2 = (f32[16,1,128]{2,0,1:T(8,128)S(1)}, f32[16,1,128]{2,0,1:T(8,128)S(1)}, u32[]{:S(2)}, u32[]{:S(2)}) collective-permute-start(f32[16,1,128]{2,0,1:T(8,128)S(1)} %slice_select_fusion.1), channel_id=1, source_target_pairs={{0,2},{2,0},{4,6},{6,4},{8,10},{10,8},{12,14},{14,12},{1,3},{3,1},... | collective-permute-start | bytes 24584 | tf_op jit(solution)/shard_map/ppermute | solution.py:18
  196.1 0.7 copy-start.4
  198.3 0.6 copy-start
  198.3 0.6 copy-start.3
Sparse Core Ops, SparseCore 0:
  181.8 5.9 reduce-scatter.1
where the time goes:
time: 207 us; the launch traced here: 206 us
  loops' own time  68.9 us (33%)
  blocking collectives  62.3 us (30%)
  local copies, waits for them, and re-layouts  31 us (15%)
  waiting for transfers between devices  14.5 us (7%)
  between operations  14.4 us (7%)
  starting transfers between devices  7 us (3%)
  other arithmetic  5.43 us (3%)
    another operation x1, loops' own time, profile_max(): best, unused = lax.scan(sweep, start, offsets)  67 us
    all_gather x1, blocking collectives, body(): lax.all_gather(positions, ('recv', 'src'), axis=1, tiled=True)  23.2 us
    all_gather x1, blocking collectives, body(): lax.all_gather(normals, ('recv', 'src'), axis=1, tiled=True)  21.7 us
    dynamic_slice x32, local copies, waits for them, and re-layouts, profile_max(): best, unused = lax.scan(sweep, start, offsets)  21.4 us
    all_gather x1, blocking collectives, body(): lax.all_gather(area, ('recv', 'src'), axis=0, tiled=True)  17.4 us
    ppermute x3, waiting for transfers between devices, partner(): return lax.ppermute(value, axis, pairs)  8.45 us
    reduce_scatter x1, waiting for transfers between devices, body(): lax.psum_scatter(partial_flux.reshape(epochs, 4, n_src, width), 'src', sc...  6.07 us
    unnamed x27, local copies, waits for them, and re-layouts  5.88 us
  transfers between devices with their start and end apart: 5, of which 4 were waited for; matrix products, arithmetic and copies ran while one was open for 1% of the time, Pallas kernels for 0%

commit v1 on v0

v1 whole, which is shorter than its diff:
```python
import functools
import math

import jax
import jax.numpy as jnp
from jax import lax
from jax.experimental import pallas as pl
from jax.experimental.pallas import tpu as pltpu
from jax.sharding import PartitionSpec as P

solar_flux = 2.0
emissivity = 0.9
surface_gain = 0.1
shade_width = 0.1
reach_offset = 0.05
tiny = 1e-30

PX, PY, PZ, NX, NY, NZ, AREA, ALBEDO, TOP, SAMPLES = range(10)
group = 8


def fourth(value):
    square = value * value
    return square * square


def row_of(ref, index, count):
    return ref[pl.ds(index, 1), :] + jnp.zeros((count, 1), jnp.float32)


def step_kernel(
    held,
    per_azimuth,
    tab_ref,
    sel_ref,
    sun_ref,
    pos_ref,
    nrm_ref,
    albedo_ref,
    cond_ref,
    soil_ref,
    final_ref,
    bounce_ref,
    ring,
    rec,
    stage,
    view,
    hz,
    rows_v,
    turn_v,
    rows_s,
    turn_s,
    load_ref,
    sems,
):
    blocks, width = tab_ref.shape[1:]
    epochs = sun_ref.shape[1]
    layers = soil_ref.shape[0]
    f32 = jnp.float32

    shift = tab_ref[SAMPLES]
    whole = jnp.maximum(jnp.ceil(shift * (1.0 / width)) - 1.0, 0.0)
    rows_v[...] = whole.astype(jnp.int32)
    turn_v[...] = (shift - whole * width).astype(jnp.int32)
    copies = [
        pltpu.make_async_copy(rows_v, rows_s, sems.at[0]),
        pltpu.make_async_copy(turn_v, turn_s, sems.at[1]),
    ]
    for copy in copies:
        copy.start()

    for axis in range(3):
        ring[axis, pl.ds(0, blocks), :] = tab_ref[axis]
        ring[axis, pl.ds(blocks, blocks), :] = tab_ref[axis]

    stage[...] = jnp.zeros_like(stage)
    stage[pl.ds(0, 3), :] = pos_ref[...]
    stage[pl.ds(3, 3), :] = -nrm_ref[...]
    columns = stage[...].T
    for item in range(6):
        rec[item] = jnp.broadcast_to(columns[:, item : item + 1], (width, width))

    def view_block(block, carry):
        src = [row_of(tab_ref.at[item], block, group) for item in range(7)]
        scale = src[AREA] * row_of(sel_ref.at[0], block, group) * (1.0 / math.pi)

        for part in range(0, width, 2 * group):
            pieces = []
            for half in range(2):
                at = pl.ds(part + half * group, group)
                dx = rec[0, at, :] - src[PX]
                dy = rec[1, at, :] - src[PY]
                dz = rec[2, at, :] - src[PZ]
                facing = jnp.maximum(
                    rec[3, at, :] * dx + rec[4, at, :] * dy + rec[5, at, :] * dz, 0.0
                )
                toward = jnp.maximum(src[NX] * dx + src[NY] * dy + src[NZ] * dz, 0.0)
                spread = dx * dx + dy * dy + dz * dz + src[AREA]
                inverse = 1.0 / spread
                pieces.append(facing * toward * scale * inverse * inverse)
            view[block, pl.ds(part, 2 * group), :] = jnp.concatenate(pieces, 0).astype(
                jnp.bfloat16
            )
        return carry

    lax.fori_loop(0, blocks, view_block, 0)

    for copy in copies:
        copy.wait()

    chunk = min(blocks, 2 * group)
    lane = lax.broadcasted_iota(jnp.int32, (chunk, width), 1)

    def azimuth(index, carry):
        line, spot = index // held, (index % held) * per_azimuth
        for low in range(0, blocks, chunk):
            here = [tab_ref[axis, pl.ds(low, chunk), :] for axis in range(3)]

            def sample(number, best):
                row = rows_s[line, spot + number] + low
                part = turn_s[line, spot + number]
                keep = lane >= part
                there = []
                for axis in range(3):
                    near = ring[axis, pl.ds(row, chunk), :]
                    far = ring[axis, pl.ds(row + 1, chunk), :]
                    there.append(pltpu.roll(jnp.where(keep, near, far), width - part, 1))
                dx = there[0] - here[0]
                dy = there[1] - here[1]
                top = there[2] - here[2]
                square = jnp.maximum(dx * dx + dy * dy, tiny)
                reach = square * lax.rsqrt(square) + reach_offset
                above = top * best[1] > best[0] * reach
                return (jnp.where(above, top, best[0]), jnp.where(above, reach, best[1]))

            start = (jnp.full((chunk, width), -1e30, f32), jnp.ones((chunk, width), f32))
            best = lax.fori_loop(0, per_azimuth, sample, start, unroll=4)
            hz[pl.ds(index * blocks + low, chunk), :] = best[0] / best[1]
        return carry

    lax.fori_loop(0, epochs, azimuth, 0)

    def source(block, carry):
        flux, own = carry
        horizon = hz[pl.ds(block, epochs, stride=blocks), :]
        src = [row_of(tab_ref.at[item], block, epochs) for item in range(NX, SAMPLES)]
        nx, ny, nz, area, albedo, top = src
        incidence = sun_ref[0] * nx + sun_ref[1] * ny + sun_ref[2] * nz
        shade = jax.nn.sigmoid((sun_ref[3] - horizon) * (1.0 / shade_width))
        direct = solar_flux * jnp.maximum(incidence, 0.0) * shade
        radiance = (albedo * direct + emissivity * fourth(top)).astype(jnp.bfloat16)
        flux = flux + lax.dot_general(
            radiance, view[block], (((1,), (1,)), ((), ())), preferred_element_type=f32
        )
        own = own + direct * row_of(sel_ref.at[1], block, epochs)
        return (flux, own)

    zero = jnp.zeros((epochs, width), f32)
    bounce, direct = lax.fori_loop(0, blocks, source, (zero, zero))
    bounce_ref[...] = bounce
    load_ref[...] = (1.0 - albedo_ref[...]) * (direct + bounce)

    count = layers // group
    slabs = tuple(soil_ref[pl.ds(slab, group, stride=count), :] for slab in range(count))
    sub = lax.broadcasted_iota(jnp.int32, (group, width), 0)
    surface = sub == 0
    inner = sub < group - 1
    cond = cond_ref[...] + jnp.zeros((group, 1), f32)

    def advance(epoch, temps):
        wrapped = pltpu.roll(temps[0], group - 1, 0)
        grads = [temps[i + 1] - temps[i] for i in range(count - 1)]
        grads.append(jnp.where(inner, wrapped - temps[-1], 0.0))
        back = jnp.where(surface, 0.0, pltpu.roll(grads[-1], 1, 0))
        changes = [grads[0] - back] + [grads[i] - grads[i - 1] for i in range(1, count)]
        temps = [temp + cond * change for temp, change in zip(temps, changes)]
        absorbed = row_of(load_ref, epoch, group)
        lit = temps[0] + surface_gain * (absorbed - emissivity * fourth(temps[0]))
        temps[0] = jnp.where(surface, lit, temps[0])
        return tuple(temps)

    slabs = lax.fori_loop(0, epochs, advance, slabs, unroll=4)
    for slab in range(count):
        final_ref[pl.ds(slab, group, stride=count), :] = slabs[slab]


def body(positions, normals, area, albedo, conductivity, soil, sun_tan, samples, occupancy):
    width = positions.shape[1]
    axes = ("recv", "src")
    blocks = lax.axis_size("recv") * lax.axis_size("src")
    me = lax.axis_index("recv") * lax.axis_size("src") + lax.axis_index("src")
    epochs = sun_tan.shape[0]
    layers = soil.shape[0]
    azimuths, per_azimuth = samples.shape
    f32 = jnp.float32

    line = jnp.zeros((1, width), f32)
    line = lax.dynamic_update_slice(line, samples.reshape(1, -1).astype(f32), (0, 0))
    tile = jnp.concatenate(
        [positions, normals, area[None], albedo[None], soil[:1], line], 0
    )
    items = tile.shape[0]
    spread = jnp.broadcast_to(tile.reshape(1, 2, items // 2 * width), (blocks, 2, items // 2 * width))
    table = lax.all_to_all(spread, axes, split_axis=0, concat_axis=0, tiled=True)
    table = jnp.transpose(table.reshape(blocks, items, width), (1, 0, 2))

    weights = lax.dynamic_slice_in_dim(occupancy, me, 1, 0).reshape(blocks, 1).astype(f32)
    mine = (jnp.arange(blocks, dtype=jnp.int32) == me).astype(f32).reshape(blocks, 1)
    select = jnp.broadcast_to(jnp.stack([weights, mine]), (2, blocks, width))

    angle = 2.0 * math.pi * jnp.arange(epochs, dtype=f32) / epochs
    level = lax.rsqrt(1.0 + sun_tan * sun_tan)
    sun = jnp.stack([level * jnp.cos(angle), level * jnp.sin(angle), level * sun_tan, sun_tan])
    sun = jnp.broadcast_to(sun[:, :, None], (4, epochs, width))

    vmem = pl.BlockSpec(memory_space=pltpu.VMEM)
    call = pl.pallas_call(
        functools.partial(step_kernel, azimuths, per_azimuth),
        out_shape=(
            jax.ShapeDtypeStruct((layers, width), f32),
            jax.ShapeDtypeStruct((epochs, width), f32),
        ),
        in_specs=[vmem] * 8,
        out_specs=(vmem, vmem),
        scratch_shapes=[
            pltpu.VMEM((3, 2 * blocks, width), f32),
            pltpu.VMEM((6, width, width), f32),
            pltpu.VMEM((8, width), f32),
            pltpu.VMEM((blocks, width, width), jnp.bfloat16),
            pltpu.VMEM((epochs * blocks, width), f32),
            pltpu.VMEM((blocks, width), jnp.int32),
            pltpu.VMEM((blocks, width), jnp.int32),
            pltpu.SMEM((blocks, width), jnp.int32),
            pltpu.SMEM((blocks, width), jnp.int32),
            pltpu.VMEM((epochs, width), f32),
            pltpu.SemaphoreType.DMA((2,)),
        ],
    )
    return call(
        table,
        select,
        sun,
        positions,
        normals,
        albedo[None],
        conductivity[None],
        soil,
    )


def solution(mesh):
    spec = ("basin", "recv", "src")
    in_specs = (
        P(None, spec),
        P(None, spec),
        P(spec),
        P(spec),
        P(spec),
        P(None, spec),
        P(),
        P(spec, None),
        P("basin", None),
    )
    out_specs = (P(None, spec), P(None, spec))
    return jax.shard_map(body, mesh=mesh, in_specs=in_specs, out_specs=out_specs, check_vma=False)
```

time: 207 us -> 38.3 us (0.19)
  loops' own time: 68.9 us -> 0 us
  blocking collectives: 62.3 us -> 0 us
  local copies, waits for them, and re-layouts: 31 us -> 4.77 us
  Pallas kernels: 0 us -> 18.7 us
  between operations: 14.4 us -> 0.71 us
  waiting for transfers between devices: 14.5 us -> 5.67 us
  other arithmetic: 5.43 us -> 0.77 us
    another operation x3 -> x0, loops' own time: 68.9 us -> none  [the longest x1 67 us: profile_max(): best, unused = lax.scan(sweep, start, offsets)]
    all_gather x3 -> x0, blocking collectives: 62.3 us -> none  [the longest x1 23.2 us: body(): lax.all_gather(positions, ('recv', 'src'), axis=1, tiled=True)]
    dynamic_slice x40 -> x0, local copies, waits for them, and re-layouts: 22.7 us -> none  [the longest x32 21.4 us: profile_max(): best, unused = lax.scan(sweep, start, offsets)]
    pallas_call x0 -> x1, Pallas kernels: none -> 18.7 us  [body(): call(table, select, sun, positions, normals, albedo[None], conductivity[N...]
    ppermute x3 -> x0, waiting for transfers between devices: 8.45 us -> none  [partner(): return lax.ppermute(value, axis, pairs)]
    reduce_scatter x1 -> x0, waiting for transfers between devices: 6.07 us -> none  [body(): lax.psum_scatter(partial_flux.reshape(epochs, 4, n_src, width), 'src', sc...]
    all_to_all x1, waiting for transfers between devices: 0.01 us -> 5.67 us  [body(): lax.all_to_all(spread, axes, split_axis=0, concat_axis=0, tiled=True)]
    all_to_all x1, starting transfers between devices: 3.47 us -> 7.41 us  [body(): lax.all_to_all(spread, axes, split_axis=0, concat_axis=0, tiled=True)]
  transfers between devices with their start and end apart: 5 -> 1, of which waited for: 4 -> 1; matrix products, arithmetic and copies ran while one was open for 1% -> 2% of each run, Pallas kernels for 0% -> 0%
where the time goes in v1:
time: 38.3 us; the launch traced here: 38 us
  Pallas kernels  18.7 us (49%)
  starting transfers between devices  7.41 us (19%)
  waiting for transfers between devices  5.67 us (15%)
  local copies, waits for them, and re-layouts  4.77 us (12%)
  other arithmetic  0.77 us (2%)
  between operations  0.71 us (2%)
    pallas_call x1, Pallas kernels, body(): call(table, select, sun, positions, normals, albedo[None], conductivity[N...  18.7 us
    all_to_all x1, starting transfers between devices, body(): lax.all_to_all(spread, axes, split_axis=0, concat_axis=0, tiled=True)  7.41 us
    all_to_all x1, waiting for transfers between devices, body(): lax.all_to_all(spread, axes, split_axis=0, concat_axis=0, tiled=True)  5.67 us
    unnamed x12, local copies, waits for them, and re-layouts  1.97 us
  transfers between devices with their start and end apart: 1, of which 1 were waited for; matrix products, arithmetic and copies ran while one was open for 2% of the time, Pallas kernels for 0%

profile of v1, /device:TPU:0, one launch (start us, length us, event | category | flops | bytes accessed | tf_op | source)
XLA Modules:
  0.0 38.0 jit_solution(8839080972400093607)
XLA Ops:
  0.6 0.0 copy-start.5
  0.6 0.6 %copy-done.5 = s32[1,32]{1,0:T(1,128)S(1)} copy-done((s32[1,32]{1,0:T(1,128)S(1)}, s32[1,32]{1,0:T(1,128)}, u32[]{:S(2)}) %copy-start.5) | copy-done | bytes 152
  1.3 0.0 copy-start.1
  1.3 0.0 copy-start
  1.3 0.0 slice-start
  1.3 0.0 copy-start.2
  1.3 0.0 copy-start.4
  1.3 0.6 %copy-done.1 = f32[3,128]{1,0:T(4,128)S(1)} copy-done((f32[3,128]{1,0:T(4,128)S(1)}, f32[3,128]{1,0:T(4,128)}, u32[]{:S(2)}) %copy-start.1) | copy-done | bytes 1560
  2.0 0.0 copy-done
  2.0 0.0 slice-done
  2.0 0.0 copy-done.2
  2.0 0.0 copy-done.4
  2.1 0.7 %broadcast_in_dim.34 = f32[16,2,640]{2,1,0:T(2,128)} broadcast(f32[2,640]{1,0:T(2,128)S(1)} %broadcast_in_dim.33), dimensions={1,2} | broadcast | bytes 87040 | tf_op jit(solution)/shard_map/broadcast_in_dim | solution.py:203
  2.7 7.4 %all-to-all-start = ((f32[16,2,640]{2,1,0:T(2,128)}), f32[16,2,640]{2,1,0:T(2,128)S(1)}, u32[]{:S(2)}, u32[]{:S(2)}) async-start(f32[16,2,640]{2,1,0:T(2,128)} %broadcast_in_dim.34), calls=%async_computation | async-start | bytes 163840 | tf_op jit(solution)/shard_map/all_to_all | solution.py:204
  10.2 0.0 copy-start.3
  10.2 0.6 %copy-done.3 = f32[16]{0:T(128)S(1)} copy-done((f32[16]{0:T(128)S(1)}, f32[16]{0:T(128)}, u32[]{:S(2)}) %copy-start.3) | copy-done | bytes 88
  10.9 0.7 %convert_bitcast_fusion = f32[1,16,1]{1,2,0:T(1,128)S(1)} fusion(s32[16,16]{1,0:T(8,128)} %param.17, s32[]{:T(128)S(6)} %select_n.3), kind=kLoop, calls=%fused_computation.9 | loop fusion | flops 16 | bytes 132 | tf_op jit(solution)/shard_map/convert_element_type | solution.py:207
  11.6 5.7 %all-to-all-done = f32[16,2,640]{2,1,0:T(2,128)S(1)} async-done(((f32[16,2,640]{2,1,0:T(2,128)}), f32[16,2,640]{2,1,0:T(2,128)S(1)}, u32[]{:S(2)}, u32[]{:S(2)}) %all-to-all-start) | async-done | bytes 81952 | tf_op jit(solution)/shard_map/all_to_all | solution.py:204
  17.3 0.1 reshape.35
  17.3 0.7 %copy.13 = f32[16,10,128]{2,0,1:T(8,128)} copy(f32[16,10,128]{2,1,0:T(8,128)S(1)} %reshape.35) | data formatting | bytes 163840 | tf_op jit(solution)/shard_map/reshape | solution.py:205
  18.0 0.7 %broadcast_in_dim.36.sel_ref = f32[2,16,128]{2,1,0:T(8,128)} broadcast(f32[2,16]{1,0:T(2,128)S(1)} %bitcast.17), dimensions={0,1} | broadcast | bytes 16512 | tf_op jit(solution)/shard_map/broadcast_in_dim | solution.py:209
  18.7 0.7 %broadcast_in_dim.37.sun_ref = f32[4,16,128]{2,1,0:T(8,128)} broadcast(f32[4,16]{1,0:T(4,128)S(1)} %pad_maximum_fusion), dimensions={0,1} | broadcast | bytes 33024 | tf_op jit(solution)/shard_map/broadcast_in_dim | solution.py:214
  19.3 18.7 %shard_map.104 = (f32[32,128]{1,0:T(8,128)}, f32[16,128]{1,0:T(8,128)}) custom-call(f32[10,16,128]{2,1,0:T(8,128)} %bitcast.16, f32[2,16,128]{2,1,0:T(8,128)} %broadcast_in_dim.36.sel_ref, f32[4,16,128]{2,1,0:T(8,128)} %broadcast_in_dim.37.sun_ref, f32[3,128]{1,0:T(4,128)} %pos_ref.1, f32[3,128]{1,0:T(4,128)} %nrm_ref.1, f32[1,128]{1,0:T(1,128)} %bitcast.18, ...), custom_call_target="tpu_custom_call" | custom-call | tf_op jit(solution)/shard_map/pallas_call | solution.py:239
  (8 shorter events, 0.1 us)
Async XLA Ops:
  0.6 0.7 %copy-start.5 = (s32[1,32]{1,0:T(1,128)S(1)}, s32[1,32]{1,0:T(1,128)}, u32[]{:S(2)}) copy-start(s32[1,32]{1,0:T(1,128)} %param.16) | copy-start | bytes 388
  1.3 0.7 %copy-start.1 = (f32[3,128]{1,0:T(4,128)S(1)}, f32[3,128]{1,0:T(4,128)}, u32[]{:S(2)}) copy-start(f32[3,128]{1,0:T(4,128)} %nrm_ref.1) | copy-start | bytes 4612
  1.3 0.7 %copy-start = (f32[3,128]{1,0:T(4,128)S(1)}, f32[3,128]{1,0:T(4,128)}, u32[]{:S(2)}) copy-start(f32[3,128]{1,0:T(4,128)} %pos_ref.1) | copy-start | bytes 4612
  1.3 0.7 %slice-start = ((f32[32,128]{1,0:T(8,128)}), f32[1,128]{1,0:T(1,128)S(1)}, s32[]{:S(2)}) async-start(f32[32,128]{1,0:T(8,128)} %soil_ref.1), calls=%async_computation.1 | async-start | bytes 1024 | tf_op jit(solution)/shard_map/slice | solution.py:200
  1.3 0.7 %copy-start.2 = (f32[128]{0:T(128)S(1)}, f32[128]{0:T(128)}, u32[]{:S(2)}) copy-start(f32[128]{0:T(128)} %param.12) | copy-start | bytes 1540
  1.3 0.7 %copy-start.4 = (f32[128]{0:T(128)S(1)}, f32[128]{0:T(128)}, u32[]{:S(2)}) copy-start(f32[128]{0:T(128)} %param.11) | copy-start | bytes 1540
  2.7 14.5 %all-to-all-start = ((f32[16,2,640]{2,1,0:T(2,128)}), f32[16,2,640]{2,1,0:T(2,128)S(1)}, u32[]{:S(2)}, u32[]{:S(2)}) async-start(f32[16,2,640]{2,1,0:T(2,128)} %broadcast_in_dim.34), calls=%async_computation | async-start | bytes 163840 | tf_op jit(solution)/shard_map/all_to_all | solution.py:204
  10.2 0.7 %copy-start.3 = (f32[16]{0:T(128)S(1)}, f32[16]{0:T(128)}, u32[]{:S(2)}) copy-start(f32[16]{0:T(128)} %param.15) | copy-start | bytes 196

commit v2 on v1

v2 whole, which is shorter than its diff:
```python
import functools
import math

import jax
import jax.numpy as jnp
from jax import lax
from jax.experimental import pallas as pl
from jax.experimental.pallas import tpu as pltpu
from jax.sharding import PartitionSpec as P

solar_flux = 2.0
emissivity = 0.9
surface_gain = 0.1
shade_width = 0.1
reach_offset = 0.05
tiny = 1e-30

PX, PY, PZ, NX, NY, NZ, AREA, ALBEDO, TOP, SAMPLES, ITEMS = range(11)
halves = 2
group = 8


def fourth(value):
    square = value * value
    return square * square


def row_of(ref, index, count):
    return ref[pl.ds(index, 1), :] + jnp.zeros((count, 1), jnp.float32)


def place_of(item, width):
    per_half = ITEMS // halves
    return item // per_half, pl.ds(item % per_half * width, width)


def pack_kernel(pos_ref, nrm_ref, area_ref, albedo_ref, soil_ref, samples_ref, out_ref, tile):
    blocks = out_ref.shape[0]
    width = pos_ref.shape[1]
    held, count = samples_ref.shape

    def put(item, value):
        half, lanes = place_of(item, width)
        tile[pl.ds(half, 1), lanes] = value

    for axis in range(3):
        put(PX + axis, pos_ref[pl.ds(axis, 1), :])
        put(NX + axis, nrm_ref[pl.ds(axis, 1), :])
    put(AREA, area_ref[...])
    put(ALBEDO, albedo_ref[...])
    put(TOP, soil_ref[pl.ds(0, 1), :])
    put(SAMPLES, jnp.zeros((1, width), jnp.float32))
    half, lanes = place_of(SAMPLES, width)
    for index in range(held):
        spot = pl.ds(lanes.start + index * count, count)
        tile[pl.ds(half, 1), spot] = samples_ref[pl.ds(index, 1), :].astype(jnp.float32)
    whole = tile[...]

    def copy(block, carry):
        out_ref[block] = whole
        return carry

    lax.fori_loop(0, blocks, copy, 0, unroll=8)


def step_kernel(
    held,
    per_azimuth,
    table_ref,
    sun_ref,
    sel_ref,
    pos_ref,
    nrm_ref,
    albedo_ref,
    cond_ref,
    soil_ref,
    final_ref,
    bounce_ref,
    tab,
    ring,
    turned,
    chosen,
    rec,
    stage,
    sun,
    sel,
    view,
    hz,
    find_v,
    find_s,
    load_ref,
    sems,
):
    blocks = table_ref.shape[0]
    width = pos_ref.shape[1]
    epochs = sun_ref.shape[1]
    layers = soil_ref.shape[0]
    f32 = jnp.float32

    stage[...] = jnp.zeros_like(stage)
    stage[0, pl.ds(0, 3), :] = pos_ref[...]
    stage[0, pl.ds(3, 3), :] = -nrm_ref[...]
    stage[1, pl.ds(0, 4), pl.ds(0, epochs)] = sun_ref[...]
    stage[1, pl.ds(4, 2), pl.ds(0, blocks)] = sel_ref[...]
    columns = stage[0].T
    others = stage[1].T

    def unpack(block, carry):
        for item in range(ITEMS):
            half, lanes = place_of(item, width)
            row = table_ref[block, pl.ds(half, 1), lanes]
            tab[item, pl.ds(block, 1), :] = row
            if item < 3:
                ring[item, pl.ds(block, 1), :] = row
                ring[item, pl.ds(blocks + block, 1), :] = row
        return carry

    lax.fori_loop(0, blocks, unpack, 0, unroll=16)

    shift = tab[SAMPLES]
    whole = jnp.maximum(jnp.ceil(shift * (1.0 / width)) - 1.0, 0.0)
    part = shift - whole * width
    double = 2 * blocks
    tabled = turned.shape[0] > group
    if tabled:
        find_v[0] = ((part - 1.0) * (3 * double) + whole).astype(jnp.int32)
    else:
        find_v[0] = whole.astype(jnp.int32)
    find_v[1] = part.astype(jnp.int32)
    lookup = pltpu.make_async_copy(find_v, find_s, sems.at[0])
    lookup.start()

    for item in range(6):
        rec[item] = jnp.broadcast_to(columns[:, item : item + 1], (width, width))
    for item in range(4):
        sun[item] = jnp.broadcast_to(others[:epochs, item : item + 1], (epochs, width))
    for item in range(2):
        sel[item] = jnp.broadcast_to(others[:blocks, item + 4 : item + 5], (blocks, width))

    chunk = min(blocks, 2 * group)
    lane = lax.broadcasted_iota(jnp.int32, (chunk, width), 1)

    def turn_rows(part, axis, near, far):
        chosen = jnp.where(lane >= part, near, far)
        return pltpu.roll(chosen, (width - part) % width, 1)

    each = -(-width // blocks)
    if tabled:
        near = [ring[axis, pl.ds(0, blocks), :] for axis in range(3)]
        far = [ring[axis, pl.ds(1, blocks), :] for axis in range(3)]
        for number in range(each * blocks):
            for axis in range(3):
                chosen[number * 3 + axis] = jnp.where(lane > number, near[axis], far[axis])

    def turn(block):
        for number in range(each):
            first = block * each + number
            for axis in range(3):
                line = pl.multiple_of((first * 3 + axis) * double, group)
                rows = pltpu.roll(chosen[first * 3 + axis], (width - 1 - first) % width, 1)
                turned[pl.ds(line, blocks), :] = rows
                turned[pl.ds(line + blocks, blocks), :] = rows

    def view_block(block, carry):
        src = [row_of(tab.at[item], block, group) for item in range(7)]
        scale = src[AREA] * row_of(sel.at[0], block, group) * (1.0 / math.pi)
        lanes = pl.ds(pl.multiple_of(block * width, width), width)
        if tabled:
            turn(block)

        for part in range(0, width, 2 * group):
            pieces = []
            for half in range(2):
                at = pl.ds(part + half * group, group)
                dx = rec[0, at, :] - src[PX]
                dy = rec[1, at, :] - src[PY]
                dz = rec[2, at, :] - src[PZ]
                facing = jnp.maximum(
                    rec[3, at, :] * dx + rec[4, at, :] * dy + rec[5, at, :] * dz, 0.0
                )
                toward = jnp.maximum(src[NX] * dx + src[NY] * dy + src[NZ] * dz, 0.0)
                spread = dx * dx + dy * dy + dz * dz + src[AREA]
                inverse = 1.0 / spread
                pieces.append(facing * toward * scale * inverse * inverse)
            view[pl.ds(part, 2 * group), lanes] = jnp.concatenate(pieces, 0).astype(jnp.bfloat16)
        return carry

    lax.fori_loop(0, blocks, view_block, 0, unroll=8)

    lookup.wait()

    def azimuth(index, carry):
        line, spot = index // held, (index % held) * per_azimuth
        for low in range(0, blocks, chunk):
            here = [tab[axis, pl.ds(low, chunk), :] for axis in range(3)]

            def sample(number, best):
                row = find_s[0, line, spot + number] + low
                if tabled:
                    there = [turned[pl.ds(row + axis * double, chunk), :] for axis in range(3)]
                else:
                    part = find_s[1, line, spot + number]
                    there = []
                    for axis in range(3):
                        near = ring[axis, pl.ds(row, chunk), :]
                        far = ring[axis, pl.ds(row + 1, chunk), :]
                        there.append(turn_rows(part, axis, near, far))
                dx = there[0] - here[0]
                dy = there[1] - here[1]
                square = jnp.maximum(dx * dx + dy * dy, tiny)
                reach = square * lax.rsqrt(square) + reach_offset
                return jnp.maximum(best, (there[2] - here[2]) / reach)

            start = jnp.full((chunk, width), -1e30, f32)
            best = lax.fori_loop(0, per_azimuth, sample, start, unroll=True)
            hz[pl.ds(index * blocks + low, chunk), :] = best
        return carry

    lax.fori_loop(0, epochs, azimuth, 0, unroll=2)

    def source(pair, carry):
        flux, own = carry
        pieces = []
        for half in range(2):
            block = 2 * pair + half
            horizon = hz[pl.ds(block, epochs, stride=blocks), :]
            src = [row_of(tab.at[item], block, epochs) for item in range(NX, SAMPLES)]
            nx, ny, nz, area, albedo, top = src
            incidence = sun[0] * nx + sun[1] * ny + sun[2] * nz
            shade = jax.nn.sigmoid((sun[3] - horizon) * (1.0 / shade_width))
            direct = solar_flux * jnp.maximum(incidence, 0.0) * shade
            radiance = albedo * direct + emissivity * fourth(top)
            pieces.append(radiance.astype(jnp.bfloat16))
            own = own + direct * row_of(sel.at[1], block, epochs)
        lanes = pl.ds(pl.multiple_of(pair * (2 * width), 2 * width), 2 * width)
        flux = flux + lax.dot_general(
            jnp.concatenate(pieces, 1),
            view[:, lanes],
            (((1,), (1,)), ((), ())),
            preferred_element_type=f32,
        )
        return (flux, own)

    zero = jnp.zeros((epochs, width), f32)
    bounce, direct = lax.fori_loop(0, blocks // 2, source, (zero, zero), unroll=8)
    bounce_ref[...] = bounce
    load_ref[...] = (1.0 - albedo_ref[...]) * (direct + bounce)

    count = layers // group
    slabs = tuple(soil_ref[pl.ds(slab, group, stride=count), :] for slab in range(count))
    sub = lax.broadcasted_iota(jnp.int32, (group, width), 0)
    surface = sub == 0
    inner = sub < group - 1
    cond = cond_ref[...] + jnp.zeros((group, 1), f32)

    def advance(epoch, temps):
        wrapped = pltpu.roll(temps[0], group - 1, 0)
        grads = [temps[i + 1] - temps[i] for i in range(count - 1)]
        grads.append(jnp.where(inner, wrapped - temps[-1], 0.0))
        back = jnp.where(surface, 0.0, pltpu.roll(grads[-1], 1, 0))
        changes = [grads[0] - back] + [grads[i] - grads[i - 1] for i in range(1, count)]
        temps = [temp + cond * change for temp, change in zip(temps, changes)]
        absorbed = row_of(load_ref, epoch, group)
        lit = temps[0] + surface_gain * (absorbed - emissivity * fourth(temps[0]))
        temps[0] = jnp.where(surface, lit, temps[0])
        return tuple(temps)

    slabs = lax.fori_loop(0, epochs, advance, slabs, unroll=8)
    for slab in range(count):
        final_ref[pl.ds(slab, group, stride=count), :] = slabs[slab]


def body(positions, normals, area, albedo, conductivity, soil, sun_tan, samples, occupancy):
    width = positions.shape[1]
    axes = ("recv", "src")
    blocks = lax.axis_size("recv") * lax.axis_size("src")
    me = lax.axis_index("recv") * lax.axis_size("src") + lax.axis_index("src")
    epochs = sun_tan.shape[0]
    layers = soil.shape[0]
    held, per_azimuth = samples.shape
    f32 = jnp.float32
    i32 = jnp.int32
    vmem = pl.BlockSpec(memory_space=pltpu.VMEM)
    half = ITEMS // halves * width

    pack = pl.pallas_call(
        pack_kernel,
        grid=(1,),
        out_shape=jax.ShapeDtypeStruct((blocks, halves, half), f32),
        in_specs=[vmem] * 4 + [pl.BlockSpec((group, width), lambda i: (0, 0)), vmem],
        out_specs=vmem,
        scratch_shapes=[pltpu.VMEM((halves, half), f32)],
        compiler_params=pltpu.CompilerParams(vmem_limit_bytes=60 * 2**20),
        name="pack",
    )
    spread = pack(positions, normals, area[None], albedo[None], soil, samples)
    table = lax.all_to_all(spread, axes, split_axis=0, concat_axis=0, tiled=True)

    weights = lax.dynamic_slice_in_dim(occupancy, me, 1, 0).astype(f32)
    mine = (jnp.arange(blocks, dtype=i32) == me).astype(f32)[None]
    select = jnp.concatenate([weights, mine], 0)

    angle = 2.0 * math.pi * jnp.arange(epochs, dtype=f32) / epochs
    level = lax.rsqrt(1.0 + sun_tan * sun_tan)
    sun = jnp.stack([level * jnp.cos(angle), level * jnp.sin(angle), level * sun_tan, sun_tan])

    each = -(-width // blocks)
    turned = each * blocks * 3 * 2 * blocks
    tabled = turned * width * 4 <= 2**24
    scratch = [
        ((ITEMS, blocks, width), f32),
        ((3, 2 * blocks, width), f32),
        ((turned if tabled else group, width), f32),
        ((each * blocks * 3, blocks, width) if tabled else (group, width), f32),
        ((6, width, width), f32),
        ((2, group, width), f32),
        ((4, epochs, width), f32),
        ((2, blocks, width), f32),
        ((width, blocks * width), jnp.bfloat16),
        ((epochs * blocks, width), f32),
        ((2, blocks, width), i32),
    ]
    held_bytes = sum(math.prod(shape) * jnp.dtype(kind).itemsize for shape, kind in scratch)
    call = pl.pallas_call(
        functools.partial(step_kernel, held, per_azimuth),
        out_shape=(
            jax.ShapeDtypeStruct((layers, width), f32),
            jax.ShapeDtypeStruct((epochs, width), f32),
        ),
        in_specs=[vmem] * 8,
        out_specs=(vmem, vmem),
        scratch_shapes=[pltpu.VMEM(*item) for item in scratch]
        + [
            pltpu.SMEM((2, blocks, width), i32),
            pltpu.VMEM((epochs, width), f32),
            pltpu.SemaphoreType.DMA((1,)),
        ],
        compiler_params=pltpu.CompilerParams(
            vmem_limit_bytes=8 * 2**20 + held_bytes * 5 // 4 + 16 * blocks * half
        ),
        name="step",
    )
    return call(
        table,
        sun,
        select,
        positions,
        normals,
        albedo[None],
        conductivity[None],
        soil,
    )


def solution(mesh):
    spec = ("basin", "recv", "src")
    in_specs = (
        P(None, spec),
        P(None, spec),
        P(spec),
        P(spec),
        P(spec),
        P(None, spec),
        P(),
        P(spec, None),
        P("basin", None),
    )
    out_specs = (P(None, spec), P(None, spec))
    return jax.shard_map(body, mesh=mesh, in_specs=in_specs, out_specs=out_specs, check_vma=False)
```

time: 38.3 us -> 21.5 us (0.56)
  Pallas kernels: 18.7 us -> 6.01 us
  local copies, waits for them, and re-layouts: 4.77 us -> 0.68 us
    pallas_call x1 -> x2, Pallas kernels: 18.7 us -> 6.01 us  [the longest x1 4.61 us: body(): call(table, sun, select, positions, normals, albedo[None], conductivity[N...]
    broadcast_in_dim x4 -> x0, local copies, waits for them, and re-layouts: 2.01 us -> none  [the longest x1 0.67 us: body(): select = jnp.broadcast_to(jnp.stack([weights, mine]), (2, blocks, width))]
    unnamed x12, local copies, waits for them, and re-layouts: 1.97 us -> 0.68 us
    reshape x2 -> x0, local copies, waits for them, and re-layouts: 0.73 us -> none  [body(): table = jnp.transpose(table.reshape(blocks, items, width), (1, 0, 2))]
  transfers between devices with their start and end apart: 1 -> 1, of which waited for: 1 -> 1; matrix products, arithmetic and copies ran while one was open for 2% -> 4% of each run, Pallas kernels for 0% -> 0%
where the time goes in v2:
time: 21.5 us; the launch traced here: 21.2 us
  starting transfers between devices  7.41 us (34%)
  Pallas kernels  6.01 us (28%)
  waiting for transfers between devices  5.6 us (26%)
  other arithmetic  0.77 us (4%)
  between operations  0.73 us (3%)
  local copies, waits for them, and re-layouts  0.68 us (3%)
    all_to_all x1, starting transfers between devices, body(): lax.all_to_all(spread, axes, split_axis=0, concat_axis=0, tiled=True)  7.41 us
    all_to_all x1, waiting for transfers between devices, body(): lax.all_to_all(spread, axes, split_axis=0, concat_axis=0, tiled=True)  5.6 us
    pallas_call x1, Pallas kernels, body(): call(table, sun, select, positions, normals, albedo[None], conductivity[N...  4.61 us
    pallas_call x1, Pallas kernels, body(): spread = pack(positions, normals, area[None], albedo[None], soil, samples)  1.41 us
    convert_element_type x1, other arithmetic, body(): weights = lax.dynamic_slice_in_dim(occupancy, me, 1, 0).astype(f32)  0.7 us
    unnamed x12, local copies, waits for them, and re-layouts  0.68 us
  transfers between devices with their start and end apart: 1, of which 1 were waited for; matrix products, arithmetic and copies ran while one was open for 4% of the time, Pallas kernels for 0%

profile of v2, /device:TPU:0, one launch (start us, length us, event | category | flops | bytes accessed | tf_op | source)
XLA Modules:
  0.0 21.2 jit_solution(11918410736754831322)
XLA Ops:
  0.6 1.4 %pack.1 = f32[16,2,640]{2,1,0:T(2,128)} custom-call(f32[3,128]{1,0:T(4,128)} %pos_ref.3, f32[3,128]{1,0:T(4,128)} %nrm_ref.3, f32[1,128]{1,0:T(1,128)} %bitcast.14, f32[1,128]{1,0:T(1,128)} %bitcast.10, f32[32,128]{1,0:T(8,128)} %soil_ref.3, s32[1,32]{1,0:T(1,128)} %samples_ref.1), custom_call_target="tpu_custom_call" | custom-call | tf_op jit(solution)/shard_map/pack/pallas_call | solution.py:296
  2.0 7.4 %all-to-all-start = ((f32[16,2,640]{2,1,0:T(2,128)}), f32[16,2,640]{2,1,0:T(2,128)S(1)}, u32[]{:S(2)}, u32[]{:S(2)}) async-start(f32[16,2,640]{2,1,0:T(2,128)} %pack.1), calls=%async_computation | async-start | bytes 163840 | tf_op jit(solution)/shard_map/all_to_all | solution.py:297
  9.5 0.0 copy-start.5
  9.5 0.6 %copy-done.5 = f32[16]{0:T(128)S(1)} copy-done((f32[16]{0:T(128)S(1)}, f32[16]{0:T(128)}, u32[]{:S(2)}) %copy-start.5) | copy-done | bytes 88
  10.2 0.0 copy-start
  10.2 0.7 %dynamic-slice_convert_fusion = f32[1,16]{1,0:T(1,128)S(1)} fusion(s32[16,16]{1,0:T(8,128)} %param.17, s32[]{:T(128)S(6)} %select_n.3), kind=kLoop, calls=%fused_computation.3 | loop fusion | flops 16 | bytes 132 | tf_op jit(solution)/shard_map/convert_element_type | solution.py:299
  10.9 0.0 copy-start.1
  10.9 0.0 copy-start.2
  10.9 0.0 copy-start.3
  11.0 0.0 copy-start.4
  11.0 5.6 %all-to-all-done.table_ref = f32[16,2,640]{2,1,0:T(2,128)S(1)} async-done(((f32[16,2,640]{2,1,0:T(2,128)}), f32[16,2,640]{2,1,0:T(2,128)S(1)}, u32[]{:S(2)}, u32[]{:S(2)}) %all-to-all-start) | async-done | bytes 81952 | tf_op jit(solution)/shard_map/all_to_all | solution.py:297
  16.6 0.0 copy-done
  16.6 0.0 copy-done.1
  16.6 0.0 copy-done.2
  16.6 0.0 copy-done.3
  16.6 0.0 copy-done.4
  16.6 4.6 %step.1 = (f32[32,128]{1,0:T(8,128)}, f32[16,128]{1,0:T(8,128)}) custom-call(f32[16,2,640]{2,1,0:T(2,128)S(1)} %all-to-all-done.table_ref, f32[4,16]{1,0:T(4,128)S(1)} %pad_maximum_fusion.sun_ref, f32[2,16]{1,0:T(2,128)S(1)} %pad_maximum_fusion.1.sel_ref, f32[3,128]{1,0:T(4,128)S(1)} %copy-done.1, f32[3,128]{1,0:T(4,128)S(1)} %copy-done.2, ...), custom_call_target="tpu_custom_call" | custom-call | tf_op jit(solution)/shard_map/step/pallas_call | solution.py:343
  (4 shorter events, 0.1 us)
Async XLA Ops:
  2.0 14.5 %all-to-all-start = ((f32[16,2,640]{2,1,0:T(2,128)}), f32[16,2,640]{2,1,0:T(2,128)S(1)}, u32[]{:S(2)}, u32[]{:S(2)}) async-start(f32[16,2,640]{2,1,0:T(2,128)} %pack.1), calls=%async_computation | async-start | bytes 163840 | tf_op jit(solution)/shard_map/all_to_all | solution.py:297
  9.5 0.7 %copy-start.5 = (f32[16]{0:T(128)S(1)}, f32[16]{0:T(128)}, u32[]{:S(2)}) copy-start(f32[16]{0:T(128)} %param.15) | copy-start | bytes 196
  10.2 6.4 %copy-start = (f32[32,128]{1,0:T(8,128)S(1)}, f32[32,128]{1,0:T(8,128)}, u32[]{:S(2)}) copy-start(f32[32,128]{1,0:T(8,128)} %soil_ref.3) | copy-start | bytes 49156
  10.9 5.7 %copy-start.1 = (f32[3,128]{1,0:T(4,128)S(1)}, f32[3,128]{1,0:T(4,128)}, u32[]{:S(2)}) copy-start(f32[3,128]{1,0:T(4,128)} %pos_ref.3) | copy-start | bytes 4612
  10.9 5.7 %copy-start.2 = (f32[3,128]{1,0:T(4,128)S(1)}, f32[3,128]{1,0:T(4,128)}, u32[]{:S(2)}) copy-start(f32[3,128]{1,0:T(4,128)} %nrm_ref.3) | copy-start | bytes 4612
  10.9 5.6 %copy-start.3 = (f32[128]{0:T(128)S(1)}, f32[128]{0:T(128)}, u32[]{:S(2)}) copy-start(f32[128]{0:T(128)} %param.12) | copy-start | bytes 1540
  11.0 5.6 %copy-start.4 = (f32[128]{0:T(128)S(1)}, f32[128]{0:T(128)}, u32[]{:S(2)}) copy-start(f32[128]{0:T(128)} %param.13) | copy-start | bytes 1540

commit v3 on v2

--- a/solution.py
+++ b/solution.py
@@ -3,6 +3,7 @@
 
 import jax
 import jax.numpy as jnp
+import numpy as np
 from jax import lax
 from jax.experimental import pallas as pl
 from jax.experimental.pallas import tpu as pltpu
@@ -34,14 +35,44 @@
     return item // per_half, pl.ds(item % per_half * width, width)
 
 
-def pack_kernel(pos_ref, nrm_ref, area_ref, albedo_ref, soil_ref, samples_ref, out_ref, tile):
-    blocks = out_ref.shape[0]
+def pack_kernel(
+    pos_hbm,
+    nrm_hbm,
+    area_hbm,
+    albedo_hbm,
+    soil_hbm,
+    samples_hbm,
+    out_ref,
+    pos_ref,
+    nrm_ref,
+    area_ref,
+    albedo_ref,
+    soil_ref,
+    samples_ref,
+    sems,
+):
     width = pos_ref.shape[1]
     held, count = samples_ref.shape
+    pairs = (
+        (pos_hbm, pos_ref),
+        (nrm_hbm, nrm_ref),
+        (area_hbm, area_ref),
+        (albedo_hbm, albedo_ref),
+        (soil_hbm.at[pl.ds(0, group), :], soil_ref),
+        (samples_hbm, samples_ref),
+    )
+    copies = [
+        pltpu.make_async_copy(source, target, sems.at[number])
+        for number, (source, target) in enumerate(pairs)
+    ]
+    for copy in copies:
+        copy.start()
+    for copy in copies:
+        copy.wait()
 
     def put(item, value):
         half, lanes = place_of(item, width)
-        tile[pl.ds(half, 1), lanes] = value
+        out_ref[0, pl.ds(half, 1), lanes] = value
 
     for axis in range(3):
         put(PX + axis, pos_ref[pl.ds(axis, 1), :])
@@ -53,69 +84,98 @@
     half, lanes = place_of(SAMPLES, width)
     for index in range(held):
         spot = pl.ds(lanes.start + index * count, count)
-        tile[pl.ds(half, 1), spot] = samples_ref[pl.ds(index, 1), :].astype(jnp.float32)
-    whole = tile[...]
-
-    def copy(block, carry):
-        out_ref[block] = whole
-        return carry
-
-    lax.fori_loop(0, blocks, copy, 0, unroll=8)
+        out_ref[0, pl.ds(half, 1), spot] = samples_ref[pl.ds(index, 1), :].astype(jnp.float32)
+
+
+def my_block():
+    return lax.axis_index("recv") * lax.axis_size("src") + lax.axis_index("src")
+
+
+def prepare_kernel(
+    pos_ref, nrm_ref, angle_ref, tan_ref, occupancy_ref, rec_ref, sun_ref, sel_ref, stage
+):
+    width = pos_ref.shape[1]
+    epochs = tan_ref.shape[1]
+    blocks = occupancy_ref.shape[1]
+    me = my_block()
+    stage[...] = jnp.zeros_like(stage)
+    stage[0, pl.ds(0, 3), :] = pos_ref[...]
+    stage[0, pl.ds(3, 3), :] = -nrm_ref[...]
+    tangent = tan_ref[...]
+    level = lax.rsqrt(1.0 + tangent * tangent)
+    stage[1, pl.ds(0, 2), pl.ds(0, epochs)] = angle_ref[...] * level
+    stage[1, pl.ds(2, 1), pl.ds(0, epochs)] = tangent * level
+    stage[1, pl.ds(3, 1), pl.ds(0, epochs)] = tangent
+    stage[1, pl.ds(4, 1), pl.ds(0, blocks)] = occupancy_ref[pl.ds(me, 1), :].astype(jnp.float32)
+    mine = lax.broadcasted_iota(jnp.int32, (1, blocks), 1) == me
+    stage[1, pl.ds(5, 1), pl.ds(0, blocks)] = mine.astype(jnp.float32)
+    columns = stage[0].T
+    others = stage[1].T
+    for item in range(6):
+        rec_ref[item] = jnp.broadcast_to(columns[:, item : item + 1], (width, width))
+    for item in range(4):
+        sun_ref[item] = jnp.broadcast_to(others[:epochs, item : item + 1], (epochs, width))
+    for item in range(2):
+        sel_ref[item] = jnp.broadcast_to(others[:blocks, item + 4 : item + 5], (blocks, width))
 
 
 def step_kernel(
     held,
     per_azimuth,
-    table_ref,
-    sun_ref,
-    sel_ref,
-    pos_ref,
-    nrm_ref,
-    albedo_ref,
-    cond_ref,
-    soil_ref,
+    masks,
+    near_ref,
+    far_ref,
+    rec,
+    sun,
+    sel,
+    albedo_hbm,
+    cond_hbm,
+    soil_hbm,
     final_ref,
     bounce_ref,
     tab,
     ring,
     turned,
     chosen,
-    rec,
-    stage,
-    sun,
-    sel,
     view,
     hz,
     find_v,
     find_s,
     load_ref,
+    albedo_ref,
+    cond_ref,
+    soil_ref,
     sems,
 ):
-    blocks = table_ref.shape[0]
-    width = pos_ref.shape[1]
-    epochs = sun_ref.shape[1]
+    pairs = ((albedo_hbm, albedo_ref), (cond_hbm, cond_ref), (soil_hbm, soil_ref))
+    late = [
+        pltpu.make_async_copy(source, target, sems.at[number])
+        for number, (source, target) in enumerate(pairs)
+    ]
+    for copy in late:
+        copy.start()
+    blocks = near_ref.shape[0] + far_ref.shape[0]
+    width = cond_ref.shape[1]
+    epochs = sun.shape[1]
     layers = soil_ref.shape[0]
     f32 = jnp.float32
-
-    stage[...] = jnp.zeros_like(stage)
-    stage[0, pl.ds(0, 3), :] = pos_ref[...]
-    stage[0, pl.ds(3, 3), :] = -nrm_ref[...]
-    stage[1, pl.ds(0, 4), pl.ds(0, epochs)] = sun_ref[...]
-    stage[1, pl.ds(4, 2), pl.ds(0, blocks)] = sel_ref[...]
-    columns = stage[0].T
-    others = stage[1].T
-
-    def unpack(block, carry):
+    me = my_block()
+
+    def unpack(ref, slot, block):
         for item in range(ITEMS):
             half, lanes = place_of(item, width)
-            row = table_ref[block, pl.ds(half, 1), lanes]
+            row = ref[slot, pl.ds(half, 1), lanes]
             tab[item, pl.ds(block, 1), :] = row
             if item < 3:
                 ring[item, pl.ds(block, 1), :] = row
                 ring[item, pl.ds(blocks + block, 1), :] = row
-        return carry
-
-    lax.fori_loop(0, blocks, unpack, 0, unroll=16)
+
+    for slot in range(blocks // 2):
+        mask = 0
+        for bit in range(len(masks) - 1):
+            mask ^= masks[bit] * (slot >> bit & 1)
+        unpack(near_ref, slot, me ^ mask)
+        unpack(far_ref, slot, me ^ mask ^ masks[-1])
 
     shift = tab[SAMPLES]
     whole = jnp.maximum(jnp.ceil(shift * (1.0 / width)) - 1.0, 0.0)
@@ -127,15 +187,8 @@
     else:
         find_v[0] = whole.astype(jnp.int32)
     find_v[1] = part.astype(jnp.int32)
-    lookup = pltpu.make_async_copy(find_v, find_s, sems.at[0])
+    lookup = pltpu.make_async_copy(find_v, find_s, sems.at[3])
     lookup.start()
-
-    for item in range(6):
-        rec[item] = jnp.broadcast_to(columns[:, item : item + 1], (width, width))
-    for item in range(4):
-        sun[item] = jnp.broadcast_to(others[:epochs, item : item + 1], (epochs, width))
-    for item in range(2):
-        sel[item] = jnp.broadcast_to(others[:blocks, item + 4 : item + 5], (blocks, width))
 
     chunk = min(blocks, 2 * group)
     lane = lax.broadcasted_iota(jnp.int32, (chunk, width), 1)
@@ -244,6 +297,8 @@
     zero = jnp.zeros((epochs, width), f32)
     bounce, direct = lax.fori_loop(0, blocks // 2, source, (zero, zero), unroll=8)
     bounce_ref[...] = bounce
+    for copy in late:
+        copy.wait()
     load_ref[...] = (1.0 - albedo_ref[...]) * (direct + bounce)
 
     count = layers // group
@@ -273,36 +328,63 @@
 def body(positions, normals, area, albedo, conductivity, soil, sun_tan, samples, occupancy):
     width = positions.shape[1]
     axes = ("recv", "src")
-    blocks = lax.axis_size("recv") * lax.axis_size("src")
-    me = lax.axis_index("recv") * lax.axis_size("src") + lax.axis_index("src")
+    n_recv, n_src = lax.axis_size("recv"), lax.axis_size("src")
+    blocks = n_recv * n_src
     epochs = sun_tan.shape[0]
     layers = soil.shape[0]
     held, per_azimuth = samples.shape
     f32 = jnp.float32
     i32 = jnp.int32
     vmem = pl.BlockSpec(memory_space=pltpu.VMEM)
+    hbm = pl.BlockSpec(memory_space=pltpu.HBM)
     half = ITEMS // halves * width
 
     pack = pl.pallas_call(
         pack_kernel,
-        grid=(1,),
-        out_shape=jax.ShapeDtypeStruct((blocks, halves, half), f32),
-        in_specs=[vmem] * 4 + [pl.BlockSpec((group, width), lambda i: (0, 0)), vmem],
+        out_shape=jax.ShapeDtypeStruct((1, halves, half), f32),
+        in_specs=[hbm] * 6,
         out_specs=vmem,
-        scratch_shapes=[pltpu.VMEM((halves, half), f32)],
-        compiler_params=pltpu.CompilerParams(vmem_limit_bytes=60 * 2**20),
+        scratch_shapes=[
+            pltpu.VMEM((3, width), f32),
+            pltpu.VMEM((3, width), f32),
+            pltpu.VMEM((1, width), f32),
+            pltpu.VMEM((1, width), f32),
+            pltpu.VMEM((group, width), f32),
+            pltpu.VMEM((held, per_azimuth), i32),
+            pltpu.SemaphoreType.DMA((6,)),
+        ],
+        compiler_params=pltpu.CompilerParams(vmem_limit_bytes=4 * 2**20),
         name="pack",
     )
-    spread = pack(positions, normals, area[None], albedo[None], soil, samples)
-    table = lax.all_to_all(spread, axes, split_axis=0, concat_axis=0, tiled=True)
-
-    weights = lax.dynamic_slice_in_dim(occupancy, me, 1, 0).astype(f32)
-    mine = (jnp.arange(blocks, dtype=i32) == me).astype(f32)[None]
-    select = jnp.concatenate([weights, mine], 0)
-
-    angle = 2.0 * math.pi * jnp.arange(epochs, dtype=f32) / epochs
-    level = lax.rsqrt(1.0 + sun_tan * sun_tan)
-    sun = jnp.stack([level * jnp.cos(angle), level * jnp.sin(angle), level * sun_tan, sun_tan])
+    in_hbm = functools.partial(pltpu.with_memory_space_constraint, memory_space=pltpu.HBM)
+    near = pack(
+        *map(in_hbm, (positions, normals, area[None], albedo[None], soil, samples))
+    )
+
+    masks = [n_src << bit | n_src - 1 for bit in reversed(range(n_recv.bit_length() - 1))]
+    masks += [1 << bit for bit in reversed(range(n_src.bit_length() - 1))]
+    far = None
+    for mask in masks:
+        if far is not None:
+            near = jnp.concatenate([near, far], 0)
+        far = lax.ppermute(near, axes, [(index, index ^ mask) for index in range(blocks)])
+
+    angle = 2.0 * math.pi * np.arange(epochs) / epochs
+    angles = jnp.asarray(np.stack([np.cos(angle), np.sin(angle)]), f32)
+    prepare = pl.pallas_call(
+        prepare_kernel,
+        out_shape=(
+            jax.ShapeDtypeStruct((6, width, width), f32),
+            jax.ShapeDtypeStruct((4, epochs, width), f32),
+            jax.ShapeDtypeStruct((2, blocks, width), f32),
+        ),
+        in_specs=[vmem] * 5,
+        out_specs=(vmem, vmem, vmem),
+        scratch_shapes=[pltpu.VMEM((2, group, width), f32)],
+        compiler_params=pltpu.CompilerParams(vmem_limit_bytes=4 * 2**20),
+        name="prepare",
+    )
+    rec, sun, sel = prepare(positions, normals, angles, sun_tan[None], occupancy)
 
     each = -(-width // blocks)
     turned = each * blocks * 3 * 2 * blocks
@@ -312,28 +394,27 @@
         ((3, 2 * blocks, width), f32),
         ((turned if tabled else group, width), f32),
         ((each * blocks * 3, blocks, width) if tabled else (group, width), f32),
-        ((6, width, width), f32),
-        ((2, group, width), f32),
-        ((4, epochs, width), f32),
-        ((2, blocks, width), f32),
         ((width, blocks * width), jnp.bfloat16),
         ((epochs * blocks, width), f32),
         ((2, blocks, width), i32),
     ]
     held_bytes = sum(math.prod(shape) * jnp.dtype(kind).itemsize for shape, kind in scratch)
     call = pl.pallas_call(
-        functools.partial(step_kernel, held, per_azimuth),
+        functools.partial(step_kernel, held, per_azimuth, masks),
         out_shape=(
             jax.ShapeDtypeStruct((layers, width), f32),
             jax.ShapeDtypeStruct((epochs, width), f32),
         ),
-        in_specs=[vmem] * 8,
+        in_specs=[vmem] * 5 + [hbm] * 3,
         out_specs=(vmem, vmem),
         scratch_shapes=[pltpu.VMEM(*item) for item in scratch]
         + [
             pltpu.SMEM((2, blocks, width), i32),
             pltpu.VMEM((epochs, width), f32),
-            pltpu.SemaphoreType.DMA((1,)),
+            pltpu.VMEM((1, width), f32),
+            pltpu.VMEM((1, width), f32),
+            pltpu.VMEM((layers, width), f32),
+            pltpu.SemaphoreType.DMA((4,)),
         ],
         compiler_params=pltpu.CompilerParams(
             vmem_limit_bytes=8 * 2**20 + held_bytes * 5 // 4 + 16 * blocks * half
@@ -341,14 +422,12 @@
         name="step",
     )
     return call(
-        table,
+        near,
+        far,
+        rec,
         sun,
-        select,
-        positions,
-        normals,
-        albedo[None],
-        conductivity[None],
-        soil,
+        sel,
+        *map(in_hbm, (albedo[None], conductivity[None], soil)),
     )
 
 

time: 21.5 us -> 19.1 us (0.89)
  waiting for transfers between devices: 5.6 us -> 4.72 us
  other arithmetic: 0.77 us -> 0.04 us
  local copies, waits for them, and re-layouts: 0.68 us -> 0.13 us
  Pallas kernels: 6.01 us -> 5.63 us
  starting transfers between devices: 7.41 us -> 7.71 us
    ppermute x0 -> x4, starting transfers between devices: none -> 7.71 us  [body(): lax.ppermute(near, axes, [(index, index ^ mask) for index in range(blocks)])]
    all_to_all x1 -> x0, starting transfers between devices: 7.41 us -> none  [body(): lax.all_to_all(spread, axes, split_axis=0, concat_axis=0, tiled=True)]
    all_to_all x1 -> x0, waiting for transfers between devices: 5.6 us -> none  [body(): lax.all_to_all(spread, axes, split_axis=0, concat_axis=0, tiled=True)]
    ppermute x0 -> x4, waiting for transfers between devices: none -> 4.72 us  [body(): lax.ppermute(near, axes, [(index, index ^ mask) for index in range(blocks)])]
    convert_element_type x2 -> x0, other arithmetic: 0.7 us -> none  [the longest x1 0.7 us: body(): weights = lax.dynamic_slice_in_dim(occupancy, me, 1, 0).astype(f32)]
    unnamed x12 -> x10, local copies, waits for them, and re-layouts: 0.68 us -> 0.13 us
    pallas_call x2 -> x3, Pallas kernels: 6.01 us -> 5.63 us  [the longest x1 4.51 us: body(): call(near, far, rec, sun, sel, *map(in_hbm, (albedo[None], conductivity[N...]
  transfers between devices with their start and end apart: 1 -> 4, of which waited for: 1 -> 4; matrix products, arithmetic and copies ran while one was open for 4% -> 0% of each run, Pallas kernels for 0% -> 2%
where the time goes in v3:
time: 19.1 us; the launch traced here: 18.9 us
  starting transfers between devices  7.71 us (40%)
  Pallas kernels  5.63 us (29%)
  waiting for transfers between devices  4.72 us (25%)
  between operations  0.68 us (4%)
    ppermute x4, starting transfers between devices, body(): lax.ppermute(near, axes, [(index, index ^ mask) for index in range(blocks)])  7.71 us
    ppermute x4, waiting for transfers between devices, body(): lax.ppermute(near, axes, [(index, index ^ mask) for index in range(blocks)])  4.72 us
    pallas_call x1, Pallas kernels, body(): call(near, far, rec, sun, sel, *map(in_hbm, (albedo[None], conductivity[N...  4.51 us
    pallas_call x1, Pallas kernels, body(): pack(*map(in_hbm, (positions, normals, area[None], albedo[None], soil, sa...  0.81 us
  transfers between devices with their start and end apart: 4, of which 4 were waited for; matrix products, arithmetic and copies ran while one was open for 0% of the time, Pallas kernels for 2%

profile of v3, /device:TPU:0, one launch (start us, length us, event | category | flops | bytes accessed | tf_op | source)
XLA Modules:
  0.0 18.9 jit_solution(17501636579297162290)
XLA Ops:
  0.6 0.8 %pack.1 = f32[1,2,640]{2,1,0:T(2,128)S(1)} custom-call(f32[3,128]{1,0:T(4,128)} %pos_ref.1, f32[3,128]{1,0:T(4,128)} %nrm_ref.1, f32[1,128]{1,0:T(1,128)} %bitcast.7, f32[1,128]{1,0:T(1,128)} %bitcast.5, f32[32,128]{1,0:T(8,128)} %soil_hbm.3, s32[1,32]{1,0:T(1,128)} %samples_hbm.1), custom_call_target="tpu_custom_call" | custom-call | tf_op jit(solution)/shard_map/pack/pallas_call | solution.py:360
  1.5 3.6 %collective-permute-start = (f32[1,2,640]{2,1,0:T(2,128)S(1)}, f32[1,2,640]{2,1,0:T(2,128)S(1)}, u32[]{:S(2)}, u32[]{:S(2)}) collective-permute-start(f32[1,2,640]{2,1,0:T(2,128)S(1)} %pack.1), channel_id=1, source_target_pairs={{0,9},{1,8},{2,11},{3,10},{4,13},{5,12},{6,15},{7,14},{8,1},{9,0},... | collective-permute-start | bytes 15368 | tf_op jit(solution)/shard_map/ppermute | solution.py:370
  5.0 1.3 %collective-permute-done = f32[1,2,640]{2,1,0:T(2,128)S(1)} collective-permute-done((f32[1,2,640]{2,1,0:T(2,128)S(1)}, f32[1,2,640]{2,1,0:T(2,128)S(1)}, u32[]{:S(2)}, u32[]{:S(2)}) %collective-permute-start) | collective-permute-done | bytes 5152 | tf_op jit(solution)/shard_map/ppermute | solution.py:370
  6.4 1.9 %collective-permute-start.1 = (f32[2,2,640]{2,1,0:T(2,128)S(1)}, f32[2,2,640]{2,1,0:T(2,128)S(1)}, u32[]{:S(2)}, u32[]{:S(2)}) collective-permute-start(f32[2,2,640]{2,1,0:T(2,128)S(1)} %pad_maximum_fusion.2), channel_id=1, source_target_pairs={{0,5},{1,4},{2,7},{3,6},{4,1},{5,0},{6,3},{7,2},{8,13},{9,12},{10,... | collective-permute-start | bytes 30728 | tf_op jit(solution)/shard_map/ppermute | solution.py:370
  8.2 1.4 %collective-permute-done.1 = f32[2,2,640]{2,1,0:T(2,128)S(1)} collective-permute-done((f32[2,2,640]{2,1,0:T(2,128)S(1)}, f32[2,2,640]{2,1,0:T(2,128)S(1)}, u32[]{:S(2)}, u32[]{:S(2)}) %collective-permute-start.1) | collective-permute-done | bytes 10272 | tf_op jit(solution)/shard_map/ppermute | solution.py:370
  9.6 0.0 copy-start
  9.7 1.7 %collective-permute-start.2 = (f32[4,2,640]{2,1,0:T(2,128)S(1)}, f32[4,2,640]{2,1,0:T(2,128)S(1)}, u32[]{:S(2)}, u32[]{:S(2)}) collective-permute-start(f32[4,2,640]{2,1,0:T(2,128)S(1)} %pad_maximum_fusion.1), channel_id=1, source_target_pairs={{0,3},{1,2},{2,1},{3,0},{4,7},{5,6},{6,5},{7,4},{8,11},{9,10},{10,... | collective-permute-start | bytes 61448 | tf_op jit(solution)/shard_map/ppermute | solution.py:370
  11.4 1.6 %collective-permute-done.2 = f32[4,2,640]{2,1,0:T(2,128)S(1)} collective-permute-done((f32[4,2,640]{2,1,0:T(2,128)S(1)}, f32[4,2,640]{2,1,0:T(2,128)S(1)}, u32[]{:S(2)}, u32[]{:S(2)}) %collective-permute-start.2) | collective-permute-done | bytes 20512 | tf_op jit(solution)/shard_map/ppermute | solution.py:370
  12.9 0.0 copy-start.1
  12.9 0.0 copy-start.2
  13.0 0.0 copy-start.3
  13.0 0.0 copy-start.4
  13.0 0.5 %collective-permute-start.3 = (f32[8,2,640]{2,1,0:T(2,128)S(1)}, f32[8,2,640]{2,1,0:T(2,128)S(1)}, u32[]{:S(2)}, u32[]{:S(2)}) collective-permute-start(f32[8,2,640]{2,1,0:T(2,128)S(1)} %pad_maximum_fusion.near_ref), channel_id=1, source_target_pairs={{0,1},{1,0},{2,3},{3,2},{4,5},{5,4},{6,7},{7,6},{8,9},{9,8},{10,11... | collective-permute-start | bytes 122888 | tf_op jit(solution)/shard_map/ppermute | solution.py:370
  13.5 0.0 copy-done
  13.5 0.1 copy-done.1
  13.6 0.0 copy-done.2
  13.6 0.0 copy-done.3
  13.6 0.0 copy-done.4
  13.6 0.3 %prepare.1 = (f32[6,128,128]{2,1,0:T(8,128)S(1)}, f32[4,16,128]{2,1,0:T(8,128)S(1)}, f32[2,16,128]{2,1,0:T(8,128)S(1)}) custom-call(f32[3,128]{1,0:T(4,128)S(1)} %copy-done.1, f32[3,128]{1,0:T(4,128)S(1)} %copy-done.2, f32[2,16]{1,0:T(2,128)S(1)} %copy-done.3, f32[1,16]{1,0:T(1,128)S(1)} %bitcast.4, s32[16,16]{1,0:T(8,128)S(1)} %copy-done), custom_call_target="tpu_custom_call" | custom-call | tf_op jit(solution)/shard_map/prepare/pallas_call | solution.py:387
  13.9 0.4 %collective-permute-done.3.far_ref = f32[8,2,640]{2,1,0:T(2,128)S(1)} collective-permute-done((f32[8,2,640]{2,1,0:T(2,128)S(1)}, f32[8,2,640]{2,1,0:T(2,128)S(1)}, u32[]{:S(2)}, u32[]{:S(2)}) %collective-permute-start.3) | collective-permute-done | bytes 40992 | tf_op jit(solution)/shard_map/ppermute | solution.py:370
  14.4 4.5 %step.1 = (f32[32,128]{1,0:T(8,128)}, f32[16,128]{1,0:T(8,128)}) custom-call(f32[8,2,640]{2,1,0:T(2,128)S(1)} %pad_maximum_fusion.near_ref, f32[8,2,640]{2,1,0:T(2,128)S(1)} %collective-permute-done.3.far_ref, f32[6,128,128]{2,1,0:T(8,128)S(1)} %get-tuple-element.5.rec, f32[4,16,128]{2,1,0:T(8,128)S(1)} %get-tuple-element.6.sun, ...), custom_call_target="tpu_custom_call" | custom-call | tf_op jit(solution)/shard_map/step/pallas_call | solution.py:424
  (3 shorter events, 0.0 us)
Async XLA Ops:
  1.5 4.9 %collective-permute-start = (f32[1,2,640]{2,1,0:T(2,128)S(1)}, f32[1,2,640]{2,1,0:T(2,128)S(1)}, u32[]{:S(2)}, u32[]{:S(2)}) collective-permute-start(f32[1,2,640]{2,1,0:T(2,128)S(1)} %pack.1), channel_id=1, source_target_pairs={{0,9},{1,8},{2,11},{3,10},{4,13},{5,12},{6,15},{7,14},{8,1},{9,0},... | collective-permute-start | bytes 15368 | tf_op jit(solution)/shard_map/ppermute | solution.py:370
  6.4 3.3 %collective-permute-start.1 = (f32[2,2,640]{2,1,0:T(2,128)S(1)}, f32[2,2,640]{2,1,0:T(2,128)S(1)}, u32[]{:S(2)}, u32[]{:S(2)}) collective-permute-start(f32[2,2,640]{2,1,0:T(2,128)S(1)} %pad_maximum_fusion.2), channel_id=1, source_target_pairs={{0,5},{1,4},{2,7},{3,6},{4,1},{5,0},{6,3},{7,2},{8,13},{9,12},{10,... | collective-permute-start | bytes 30728 | tf_op jit(solution)/shard_map/ppermute | solution.py:370
  9.6 3.9 %copy-start = (s32[16,16]{1,0:T(8,128)S(1)}, s32[16,16]{1,0:T(8,128)}, u32[]{:S(2)}) copy-start(s32[16,16]{1,0:T(8,128)} %occupancy_ref.1) | copy-start | bytes 3076
  9.7 3.3 %collective-permute-start.2 = (f32[4,2,640]{2,1,0:T(2,128)S(1)}, f32[4,2,640]{2,1,0:T(2,128)S(1)}, u32[]{:S(2)}, u32[]{:S(2)}) collective-permute-start(f32[4,2,640]{2,1,0:T(2,128)S(1)} %pad_maximum_fusion.1), channel_id=1, source_target_pairs={{0,3},{1,2},{2,1},{3,0},{4,7},{5,6},{6,5},{7,4},{8,11},{9,10},{10,... | collective-permute-start | bytes 61448 | tf_op jit(solution)/shard_map/ppermute | solution.py:370
  12.9 0.7 %copy-start.1 = (f32[3,128]{1,0:T(4,128)S(1)}, f32[3,128]{1,0:T(4,128)}, u32[]{:S(2)}) copy-start(f32[3,128]{1,0:T(4,128)} %pos_ref.1) | copy-start | bytes 4612
  12.9 0.7 %copy-start.2 = (f32[3,128]{1,0:T(4,128)S(1)}, f32[3,128]{1,0:T(4,128)}, u32[]{:S(2)}) copy-start(f32[3,128]{1,0:T(4,128)} %nrm_ref.1) | copy-start | bytes 4612
  13.0 0.7 %copy-start.3 = (f32[2,16]{1,0:T(2,128)S(1)}, f32[2,16]{1,0:T(2,128)}, u32[]{:S(2)}) copy-start(f32[2,16]{1,0:T(2,128)} %constant.2.clone.angle_ref) | copy-start | bytes 388
  13.0 0.7 %copy-start.4 = (f32[16]{0:T(128)S(1)}, f32[16]{0:T(128)}, u32[]{:S(2)}) copy-start(f32[16]{0:T(128)} %param.16) | copy-start | bytes 196
  13.0 1.4 %collective-permute-start.3 = (f32[8,2,640]{2,1,0:T(2,128)S(1)}, f32[8,2,640]{2,1,0:T(2,128)S(1)}, u32[]{:S(2)}, u32[]{:S(2)}) collective-permute-start(f32[8,2,640]{2,1,0:T(2,128)S(1)} %pad_maximum_fusion.near_ref), channel_id=1, source_target_pairs={{0,1},{1,0},{2,3},{3,2},{4,5},{5,4},{6,7},{7,6},{8,9},{9,8},{10,11... | collective-permute-start | bytes 122888 | tf_op jit(solution)/shard_map/ppermute | solution.py:370

commit v4 on v3

--- a/solution.py
+++ b/solution.py
@@ -15,6 +15,7 @@
 shade_width = 0.1
 reach_offset = 0.05
 tiny = 1e-30
+table_unit = 28672.0
 
 PX, PY, PZ, NX, NY, NZ, AREA, ALBEDO, TOP, SAMPLES, ITEMS = range(11)
 halves = 2
@@ -107,16 +108,58 @@
     stage[1, pl.ds(2, 1), pl.ds(0, epochs)] = tangent * level
     stage[1, pl.ds(3, 1), pl.ds(0, epochs)] = tangent
     stage[1, pl.ds(4, 1), pl.ds(0, blocks)] = occupancy_ref[pl.ds(me, 1), :].astype(jnp.float32)
-    mine = lax.broadcasted_iota(jnp.int32, (1, blocks), 1) == me
-    stage[1, pl.ds(5, 1), pl.ds(0, blocks)] = mine.astype(jnp.float32)
     columns = stage[0].T
     others = stage[1].T
     for item in range(6):
         rec_ref[item] = jnp.broadcast_to(columns[:, item : item + 1], (width, width))
     for item in range(4):
         sun_ref[item] = jnp.broadcast_to(others[:epochs, item : item + 1], (epochs, width))
-    for item in range(2):
-        sel_ref[item] = jnp.broadcast_to(others[:blocks, item + 4 : item + 5], (blocks, width))
+    sel_ref[...] = jnp.broadcast_to(others[:blocks, 4:5], (blocks, width))
+
+
+def put_views(view, first, src, weight, rec):
+    width = rec.shape[1]
+    scale = src[AREA] * weight * (1.0 / math.pi)
+    lanes = pl.ds(first, width)
+    for part in range(0, width, 2 * group):
+        pieces = []
+        for half in range(2):
+            at = pl.ds(part + half * group, group)
+            dx = rec[0, at, :] - src[PX]
+            dy = rec[1, at, :] - src[PY]
+            dz = rec[2, at, :] - src[PZ]
+            facing = jnp.maximum(
+                rec[3, at, :] * dx + rec[4, at, :] * dy + rec[5, at, :] * dz, 0.0
+            )
+            toward = jnp.maximum(src[NX] * dx + src[NY] * dy + src[NZ] * dz, 0.0)
+            spread = dx * dx + dy * dy + dz * dz + src[AREA]
+            inverse = 1.0 / spread
+            pieces.append(facing * toward * scale * inverse * inverse)
+        view[pl.ds(part, 2 * group), lanes] = jnp.concatenate(pieces, 0).astype(jnp.bfloat16)
+
+
+def origin_of(slot, masks):
+    mask = jnp.int32(0)
+    for bit in range(len(masks)):
+        mask = mask ^ masks[bit] * (slot >> bit & 1)
+    return mask
+
+
+def view_kernel(masks, near_ref, rec, sel, view):
+    width = rec.shape[1]
+    me = my_block()
+    blank = jnp.zeros((group, 1), jnp.float32)
+
+    def block_views(slot, carry):
+        src = []
+        for item in range(7):
+            half, lanes = place_of(item, width)
+            src.append(near_ref[slot, pl.ds(half, 1), lanes] + blank)
+        weight = row_of(sel, me ^ origin_of(slot, masks), group)
+        put_views(view, pl.multiple_of(slot * width, width), src, weight, rec)
+        return carry
+
+    lax.fori_loop(0, near_ref.shape[0], block_views, 0, unroll=2)
 
 
 def step_kernel(
@@ -125,6 +168,7 @@
     masks,
     near_ref,
     far_ref,
+    near_view,
     rec,
     sun,
     sel,
@@ -134,11 +178,15 @@
     final_ref,
     bounce_ref,
     tab,
+    spot_ref,
     ring,
+    flat_ring,
     turned,
     chosen,
+    flat_chosen,
     view,
-    hz,
+    lit,
+    glow,
     find_v,
     find_s,
     load_ref,
@@ -166,16 +214,14 @@
             half, lanes = place_of(item, width)
             row = ref[slot, pl.ds(half, 1), lanes]
             tab[item, pl.ds(block, 1), :] = row
-            if item < 3:
-                ring[item, pl.ds(block, 1), :] = row
-                ring[item, pl.ds(blocks + block, 1), :] = row
-
-    for slot in range(blocks // 2):
-        mask = 0
-        for bit in range(len(masks) - 1):
-            mask ^= masks[bit] * (slot >> bit & 1)
-        unpack(near_ref, slot, me ^ mask)
-        unpack(far_ref, slot, me ^ mask ^ masks[-1])
+
+    def unpack_pair(slot, carry):
+        block = me ^ origin_of(slot, masks)
+        unpack(near_ref, slot, block)
+        unpack(far_ref, slot, block ^ masks[-1])
+        return carry
+
+    lax.fori_loop(0, blocks // 2, unpack_pair, 0, unroll=8)
 
     shift = tab[SAMPLES]
     whole = jnp.maximum(jnp.ceil(shift * (1.0 / width)) - 1.0, 0.0)
@@ -193,59 +239,73 @@
     chunk = min(blocks, 2 * group)
     lane = lax.broadcasted_iota(jnp.int32, (chunk, width), 1)
 
-    def turn_rows(part, axis, near, far):
-        chosen = jnp.where(lane >= part, near, far)
-        return pltpu.roll(chosen, (width - part) % width, 1)
-
+    def turn_rows(part, near, far):
+        rows = jnp.where(lane >= part, near, far)
+        return pltpu.roll(rows, (width - part) % width, 1)
+
+    unit = table_unit if tabled else 1.0
     each = -(-width // blocks)
     if tabled:
-        near = [ring[axis, pl.ds(0, blocks), :] for axis in range(3)]
-        far = [ring[axis, pl.ds(1, blocks), :] for axis in range(3)]
-        for number in range(each * blocks):
-            for axis in range(3):
-                chosen[number * 3 + axis] = jnp.where(lane > number, near[axis], far[axis])
+        east, north = [
+            jnp.floor(tab[axis] * unit + 0.5).astype(jnp.int32) for axis in (PX, PY)
+        ]
+        spot_ref[0] = east.astype(f32)
+        spot_ref[1] = north.astype(f32)
+        spot_ref[2] = tab[PZ] * unit
+        for first in (0, blocks):
+            flat_ring[pl.ds(first, blocks), :] = (east << 16) | (north & 0xFFFF)
+            ring[pl.ds(first, blocks), :] = spot_ref[2]
+        near_flat, far_flat = [flat_ring[pl.ds(first, blocks), :] for first in (0, 1)]
+        near_top, far_top = [ring[pl.ds(first, blocks), :] for first in (0, 1)]
+
+        def choose(number, carry):
+            keep = lane > number
+            flat_chosen[number] = jnp.where(keep, near_flat, far_flat)
+            chosen[number] = jnp.where(keep, near_top, far_top)
+            return carry
+
+        lax.fori_loop(0, each * blocks, choose, 0, unroll=16)
+    else:
+        for axis in range(3):
+            spot_ref[axis] = tab[axis]
+            for first in (0, blocks):
+                line = 2 * blocks * axis + first
+                ring[pl.ds(line, blocks), :] = tab[axis]
 
     def turn(block):
         for number in range(each):
             first = block * each + number
-            for axis in range(3):
+            amount = (width - 1 - first) % width
+            flat = pltpu.roll(flat_chosen[first], amount, 1)
+            top = pltpu.roll(chosen[first], amount, 1)
+            east = (flat >> 16).astype(f32)
+            north = ((flat << 16) >> 16).astype(f32)
+            for axis, rows in enumerate((east, north, top)):
                 line = pl.multiple_of((first * 3 + axis) * double, group)
-                rows = pltpu.roll(chosen[first * 3 + axis], (width - 1 - first) % width, 1)
                 turned[pl.ds(line, blocks), :] = rows
                 turned[pl.ds(line + blocks, blocks), :] = rows
-
-    def view_block(block, carry):
+        return jnp.where(east[:group] > 2.0 * table_unit, 1.0, 0.0)
+
+    def view_block(slot, carry):
+        block = me ^ origin_of(slot + blocks // 2, masks)
         src = [row_of(tab.at[item], block, group) for item in range(7)]
-        scale = src[AREA] * row_of(sel.at[0], block, group) * (1.0 / math.pi)
-        lanes = pl.ds(pl.multiple_of(block * width, width), width)
+        weight = row_of(sel, block, group)
         if tabled:
-            turn(block)
-
-        for part in range(0, width, 2 * group):
-            pieces = []
-            for half in range(2):
-                at = pl.ds(part + half * group, group)
-                dx = rec[0, at, :] - src[PX]
-                dy = rec[1, at, :] - src[PY]
-                dz = rec[2, at, :] - src[PZ]
-                facing = jnp.maximum(
-                    rec[3, at, :] * dx + rec[4, at, :] * dy + rec[5, at, :] * dz, 0.0
-                )
-                toward = jnp.maximum(src[NX] * dx + src[NY] * dy + src[NZ] * dz, 0.0)
-                spread = dx * dx + dy * dy + dz * dz + src[AREA]
-                inverse = 1.0 / spread
-                pieces.append(facing * toward * scale * inverse * inverse)
-            view[pl.ds(part, 2 * group), lanes] = jnp.concatenate(pieces, 0).astype(jnp.bfloat16)
+            src[PX] = src[PX] + carry
+            carry = turn(2 * slot)
+            turn(2 * slot + 1)
+        put_views(view, pl.multiple_of(slot * width, width), src, weight, rec)
         return carry
 
-    lax.fori_loop(0, blocks, view_block, 0, unroll=8)
+    lax.fori_loop(0, blocks // 2, view_block, jnp.zeros((group, width), f32), unroll=4)
 
     lookup.wait()
 
     def azimuth(index, carry):
         line, spot = index // held, (index % held) * per_azimuth
+        towards = [row_of(sun.at[item], index, chunk) for item in range(4)]
         for low in range(0, blocks, chunk):
-            here = [tab[axis, pl.ds(low, chunk), :] for axis in range(3)]
+            here = [spot_ref[axis, pl.ds(low, chunk), :] for axis in range(3)]
 
             def sample(number, best):
                 row = find_s[0, line, spot + number] + low
@@ -255,57 +315,60 @@
                     part = find_s[1, line, spot + number]
                     there = []
                     for axis in range(3):
-                        near = ring[axis, pl.ds(row, chunk), :]
-                        far = ring[axis, pl.ds(row + 1, chunk), :]
-                        there.append(turn_rows(part, axis, near, far))
+                        near = ring[pl.ds(row + axis * double, chunk), :]
+                        far = ring[pl.ds(row + 1 + axis * double, chunk), :]
+                        there.append(turn_rows(part, near, far))
                 dx = there[0] - here[0]
                 dy = there[1] - here[1]
-                square = jnp.maximum(dx * dx + dy * dy, tiny)
-                reach = square * lax.rsqrt(square) + reach_offset
+                square = jnp.maximum(dx * dx + dy * dy, tiny * unit * unit)
+                reach = square * lax.rsqrt(square) + reach_offset * unit
                 return jnp.maximum(best, (there[2] - here[2]) / reach)
 
             start = jnp.full((chunk, width), -1e30, f32)
-            best = lax.fori_loop(0, per_azimuth, sample, start, unroll=True)
-            hz[pl.ds(index * blocks + low, chunk), :] = best
+            horizon = lax.fori_loop(0, per_azimuth, sample, start, unroll=True)
+            nx, ny, nz, area, albedo, top = [
+                tab[item, pl.ds(low, chunk), :] for item in range(NX, SAMPLES)
+            ]
+            incidence = towards[0] * nx + towards[1] * ny + towards[2] * nz
+            shade = jax.nn.sigmoid((towards[3] - horizon) * (1.0 / shade_width))
+            direct = solar_flux * jnp.maximum(incidence, 0.0) * shade
+            rows = pl.ds(pl.multiple_of(index * blocks + low, group), chunk)
+            lit[rows, :] = direct
+            glow[rows, :] = albedo * direct + emissivity * fourth(top)
         return carry
 
-    lax.fori_loop(0, epochs, azimuth, 0, unroll=2)
-
-    def source(pair, carry):
-        flux, own = carry
-        pieces = []
-        for half in range(2):
-            block = 2 * pair + half
-            horizon = hz[pl.ds(block, epochs, stride=blocks), :]
-            src = [row_of(tab.at[item], block, epochs) for item in range(NX, SAMPLES)]
-            nx, ny, nz, area, albedo, top = src
-            incidence = sun[0] * nx + sun[1] * ny + sun[2] * nz
-            shade = jax.nn.sigmoid((sun[3] - horizon) * (1.0 / shade_width))
-            direct = solar_flux * jnp.maximum(incidence, 0.0) * shade
-            radiance = albedo * direct + emissivity * fourth(top)
-            pieces.append(radiance.astype(jnp.bfloat16))
-            own = own + direct * row_of(sel.at[1], block, epochs)
-        lanes = pl.ds(pl.multiple_of(pair * (2 * width), 2 * width), 2 * width)
-        flux = flux + lax.dot_general(
-            jnp.concatenate(pieces, 1),
-            view[:, lanes],
-            (((1,), (1,)), ((), ())),
-            preferred_element_type=f32,
-        )
-        return (flux, own)
+    lax.fori_loop(0, epochs, azimuth, 0, unroll=8)
+
+    def source(pair, flux):
+        for views, first in ((near_view, 0), (view, blocks // 2)):
+            pieces = []
+            for half in range(2):
+                block = me ^ origin_of(first + 2 * pair + half, masks)
+                piece = glow[pl.ds(block, epochs, stride=blocks), :]
+                pieces.append(piece.astype(jnp.bfloat16))
+            lanes = pl.ds(pl.multiple_of(pair * (2 * width), 2 * width), 2 * width)
+            flux = flux + lax.dot_general(
+                jnp.concatenate(pieces, 1),
+                views[:, lanes],
+                (((1,), (1,)), ((), ())),
+                preferred_element_type=f32,
+            )
+        return flux
 
     zero = jnp.zeros((epochs, width), f32)
-    bounce, direct = lax.fori_loop(0, blocks // 2, source, (zero, zero), unroll=8)
+    bounce = lax.fori_loop(0, blocks // 4, source, zero, unroll=4)
     bounce_ref[...] = bounce
     for copy in late:
         copy.wait()
-    load_ref[...] = (1.0 - albedo_ref[...]) * (direct + bounce)
+    direct = lit[pl.ds(me, epochs, stride=blocks), :]
+    load_ref[...] = (surface_gain * (1.0 - albedo_ref[...])) * (direct + bounce)
 
     count = layers // group
     slabs = tuple(soil_ref[pl.ds(slab, group, stride=count), :] for slab in range(count))
     sub = lax.broadcasted_iota(jnp.int32, (group, width), 0)
     surface = sub == 0
     inner = sub < group - 1
+    loss = jnp.where(surface, surface_gain * emissivity, 0.0)
     cond = cond_ref[...] + jnp.zeros((group, 1), f32)
 
     def advance(epoch, temps):
@@ -315,9 +378,8 @@
         back = jnp.where(surface, 0.0, pltpu.roll(grads[-1], 1, 0))
         changes = [grads[0] - back] + [grads[i] - grads[i - 1] for i in range(1, count)]
         temps = [temp + cond * change for temp, change in zip(temps, changes)]
-        absorbed = row_of(load_ref, epoch, group)
-        lit = temps[0] + surface_gain * (absorbed - emissivity * fourth(temps[0]))
-        temps[0] = jnp.where(surface, lit, temps[0])
+        absorbed = jnp.where(surface, row_of(load_ref, epoch, group), 0.0)
+        temps[0] = (temps[0] + absorbed) - loss * fourth(temps[0])
         return tuple(temps)
 
     slabs = lax.fori_loop(0, epochs, advance, slabs, unroll=8)
@@ -361,14 +423,6 @@
         *map(in_hbm, (positions, normals, area[None], albedo[None], soil, samples))
     )
 
-    masks = [n_src << bit | n_src - 1 for bit in reversed(range(n_recv.bit_length() - 1))]
-    masks += [1 << bit for bit in reversed(range(n_src.bit_length() - 1))]
-    far = None
-    for mask in masks:
-        if far is not None:
-            near = jnp.concatenate([near, far], 0)
-        far = lax.ppermute(near, axes, [(index, index ^ mask) for index in range(blocks)])
-
     angle = 2.0 * math.pi * np.arange(epochs) / epochs
     angles = jnp.asarray(np.stack([np.cos(angle), np.sin(angle)]), f32)
     prepare = pl.pallas_call(
@@ -376,7 +430,7 @@
         out_shape=(
             jax.ShapeDtypeStruct((6, width, width), f32),
             jax.ShapeDtypeStruct((4, epochs, width), f32),
-            jax.ShapeDtypeStruct((2, blocks, width), f32),
+            jax.ShapeDtypeStruct((blocks, width), f32),
         ),
         in_specs=[vmem] * 5,
         out_specs=(vmem, vmem, vmem),
@@ -386,15 +440,39 @@
     )
     rec, sun, sel = prepare(positions, normals, angles, sun_tan[None], occupancy)
 
+    masks = [n_src << bit | n_src - 1 for bit in reversed(range(n_recv.bit_length() - 1))]
+    masks += [1 << bit for bit in reversed(range(n_src.bit_length() - 1))]
+    far = None
+    for number, mask in enumerate(masks):
+        if far is not None:
+            near = jnp.concatenate([near, far], 0)
+        if number == 2:
+            near, rec, sun, sel = lax.optimization_barrier((near, rec, sun, sel))
+        far = lax.ppermute(near, axes, [(index, index ^ mask) for index in range(blocks)])
+
+    look = pl.pallas_call(
+        functools.partial(view_kernel, masks),
+        out_shape=jax.ShapeDtypeStruct((width, blocks // 2 * width), jnp.bfloat16),
+        in_specs=[vmem] * 3,
+        out_specs=vmem,
+        compiler_params=pltpu.CompilerParams(vmem_limit_bytes=2**20),
+        name="views",
+    )
+    near_view = look(near, rec, sel)
+
     each = -(-width // blocks)
     turned = each * blocks * 3 * 2 * blocks
     tabled = turned * width * 4 <= 2**24
     scratch = [
         ((ITEMS, blocks, width), f32),
-        ((3, 2 * blocks, width), f32),
+        ((3, blocks, width), f32),
+        ((2 * blocks * (1 if tabled else 3), width), f32),
+        ((2 * blocks, width), i32),
         ((turned if tabled else group, width), f32),
-        ((each * blocks * 3, blocks, width) if tabled else (group, width), f32),
-        ((width, blocks * width), jnp.bfloat16),
+        ((each * blocks, blocks, width) if tabled else (group, width), f32),
+        ((each * blocks, blocks, width) if tabled else (group, width), i32),
+        ((width, blocks // 2 * width), jnp.bfloat16),
+        ((epochs * blocks, width), f32),
         ((epochs * blocks, width), f32),
         ((2, blocks, width), i32),
     ]
@@ -405,7 +483,7 @@
             jax.ShapeDtypeStruct((layers, width), f32),
             jax.ShapeDtypeStruct((epochs, width), f32),
         ),
-        in_specs=[vmem] * 5 + [hbm] * 3,
+        in_specs=[vmem] * 6 + [hbm] * 3,
         out_specs=(vmem, vmem),
         scratch_shapes=[pltpu.VMEM(*item) for item in scratch]
         + [
@@ -424,6 +502,7 @@
     return call(
         near,
         far,
+        near_view,
         rec,
         sun,
         sel,

time: 19.1 us -> 18.8 us (0.984)
  waiting for transfers between devices: 4.72 us -> 4.29 us
  Pallas kernels: 5.63 us -> 5.86 us
    ppermute x4, waiting for transfers between devices: 4.72 us -> 4.29 us  [body(): lax.ppermute(near, axes, [(index, index ^ mask) for index in range(blocks)])]
    pallas_call x1 -> x2, Pallas kernels: 4.51 us -> 4.73 us  [the longest x1 4.22 us: body(): call(near, far, near_view, rec, sun, sel, *map(in_hbm, (albedo[None], con...]
  transfers between devices with their start and end apart: 4 -> 4, of which waited for: 4 -> 4; matrix products, arithmetic and copies ran while one was open for 0% -> 0% of each run, Pallas kernels for 2% -> 4%
where the time goes in v4:
time: 18.8 us; the launch traced here: 18.6 us
  starting transfers between devices  7.71 us (41%)
  Pallas kernels  5.86 us (31%)
  waiting for transfers between devices  4.29 us (23%)
  between operations  0.69 us (4%)
    ppermute x4, starting transfers between devices, body(): lax.ppermute(near, axes, [(index, index ^ mask) for index in range(blocks)])  7.71 us
    ppermute x4, waiting for transfers between devices, body(): lax.ppermute(near, axes, [(index, index ^ mask) for index in range(blocks)])  4.29 us
    pallas_call x1, Pallas kernels, body(): call(near, far, near_view, rec, sun, sel, *map(in_hbm, (albedo[None], con...  4.22 us
    pallas_call x1, Pallas kernels, body(): pack(*map(in_hbm, (positions, normals, area[None], albedo[None], soil, sa...  0.81 us
    pallas_call x1, Pallas kernels, body(): near_view = look(near, rec, sel)  0.52 us
  transfers between devices with their start and end apart: 4, of which 4 were waited for; matrix products, arithmetic and copies ran while one was open for 0% of the time, Pallas kernels for 4%

profile of v4, /device:TPU:0, one launch (start us, length us, event | category | flops | bytes accessed | tf_op | source)
XLA Modules:
  0.0 18.6 jit_solution(2673648700614568008)
XLA Ops:
  0.6 0.8 %pack.1 = f32[1,2,640]{2,1,0:T(2,128)S(1)} custom-call(f32[3,128]{1,0:T(4,128)} %pos_ref.1, f32[3,128]{1,0:T(4,128)} %nrm_ref.1, f32[1,128]{1,0:T(1,128)} %bitcast.8, f32[1,128]{1,0:T(1,128)} %bitcast.5, f32[32,128]{1,0:T(8,128)} %soil_hbm.3, s32[1,32]{1,0:T(1,128)} %samples_hbm.1), custom_call_target="tpu_custom_call" | custom-call | tf_op jit(solution)/shard_map/pack/pallas_call | solution.py:422
  1.5 0.0 copy-start
  1.5 3.6 %collective-permute-start = (f32[1,2,640]{2,1,0:T(2,128)S(1)}, f32[1,2,640]{2,1,0:T(2,128)S(1)}, u32[]{:S(2)}, u32[]{:S(2)}) collective-permute-start(f32[1,2,640]{2,1,0:T(2,128)S(1)} %pack.1), channel_id=1, source_target_pairs={{0,9},{1,8},{2,11},{3,10},{4,13},{5,12},{6,15},{7,14},{8,1},{9,0},... | collective-permute-start | bytes 15368 | tf_op jit(solution)/shard_map/ppermute | solution.py:451
  5.0 1.3 %collective-permute-done = f32[1,2,640]{2,1,0:T(2,128)S(1)} collective-permute-done((f32[1,2,640]{2,1,0:T(2,128)S(1)}, f32[1,2,640]{2,1,0:T(2,128)S(1)}, u32[]{:S(2)}, u32[]{:S(2)}) %collective-permute-start) | collective-permute-done | bytes 5152 | tf_op jit(solution)/shard_map/ppermute | solution.py:451
  6.4 0.0 copy-start.1
  6.4 0.0 copy-start.2
  6.4 0.0 copy-start.3
  6.4 0.0 copy-start.4
  6.4 1.9 %collective-permute-start.1 = (f32[2,2,640]{2,1,0:T(2,128)S(1)}, f32[2,2,640]{2,1,0:T(2,128)S(1)}, u32[]{:S(2)}, u32[]{:S(2)}) collective-permute-start(f32[2,2,640]{2,1,0:T(2,128)S(1)} %pad_maximum_fusion.1), channel_id=1, source_target_pairs={{0,5},{1,4},{2,7},{3,6},{4,1},{5,0},{6,3},{7,2},{8,13},{9,12},{10,... | collective-permute-start | bytes 30728 | tf_op jit(solution)/shard_map/ppermute | solution.py:451
  8.3 0.0 copy-done
  8.4 0.0 copy-done.1
  8.4 0.0 copy-done.2
  8.4 0.0 copy-done.3
  8.4 0.0 copy-done.4
  8.4 0.3 %prepare.1 = (f32[6,128,128]{2,1,0:T(8,128)S(1)}, f32[4,16,128]{2,1,0:T(8,128)S(1)}, f32[16,128]{1,0:T(8,128)S(1)}) custom-call(f32[3,128]{1,0:T(4,128)S(1)} %copy-done.1, f32[3,128]{1,0:T(4,128)S(1)} %copy-done.2, f32[2,16]{1,0:T(2,128)S(1)} %copy-done.3, f32[1,16]{1,0:T(1,128)S(1)} %bitcast.4, s32[16,16]{1,0:T(8,128)S(1)} %copy-done), custom_call_target="tpu_custom_call" | custom-call | tf_op jit(solution)/shard_map/prepare/pallas_call | solution.py:441
  8.7 1.1 %collective-permute-done.1 = f32[2,2,640]{2,1,0:T(2,128)S(1)} collective-permute-done((f32[2,2,640]{2,1,0:T(2,128)S(1)}, f32[2,2,640]{2,1,0:T(2,128)S(1)}, u32[]{:S(2)}, u32[]{:S(2)}) %collective-permute-start.1) | collective-permute-done | bytes 10272 | tf_op jit(solution)/shard_map/ppermute | solution.py:451
  9.7 1.7 %collective-permute-start.2 = (f32[4,2,640]{2,1,0:T(2,128)S(1)}, f32[4,2,640]{2,1,0:T(2,128)S(1)}, u32[]{:S(2)}, u32[]{:S(2)}) collective-permute-start(f32[4,2,640]{2,1,0:T(2,128)S(1)} %pad_maximum_fusion), channel_id=1, source_target_pairs={{0,3},{1,2},{2,1},{3,0},{4,7},{5,6},{6,5},{7,4},{8,11},{9,10},{10,... | collective-permute-start | bytes 61448 | tf_op jit(solution)/shard_map/ppermute | solution.py:451
  11.5 1.5 %collective-permute-done.2 = f32[4,2,640]{2,1,0:T(2,128)S(1)} collective-permute-done((f32[4,2,640]{2,1,0:T(2,128)S(1)}, f32[4,2,640]{2,1,0:T(2,128)S(1)}, u32[]{:S(2)}, u32[]{:S(2)}) %collective-permute-start.2) | collective-permute-done | bytes 20512 | tf_op jit(solution)/shard_map/ppermute | solution.py:451
  13.0 0.5 %collective-permute-start.3 = (f32[8,2,640]{2,1,0:T(2,128)S(1)}, f32[8,2,640]{2,1,0:T(2,128)S(1)}, u32[]{:S(2)}, u32[]{:S(2)}) collective-permute-start(f32[8,2,640]{2,1,0:T(2,128)S(1)} %constant_dynamic-update-slice_fusion.near_ref), channel_id=1, source_target_pairs={{0,1},{1,0},{2,3},{3,2},{4,5},{5,4},{6,7},{7,6},{8,9},{9,8},{10,11... | collective-permute-start | bytes 122888 | tf_op jit(solution)/shard_map/ppermute | solution.py:451
  13.5 0.5 %views.1.near_view = bf16[128,1024]{1,0:T(8,128)(2,1)S(1)} custom-call(f32[8,2,640]{2,1,0:T(2,128)S(1)} %constant_dynamic-update-slice_fusion.near_ref, f32[6,128,128]{2,1,0:T(8,128)S(1)} %get-tuple-element.13.rec, f32[16,128]{1,0:T(8,128)S(1)} %get-tuple-element.14.sel), custom_call_target="tpu_custom_call" | custom-call | tf_op jit(solution)/shard_map/views/pallas_call | solution.py:461
  14.0 0.4 %collective-permute-done.3.far_ref = f32[8,2,640]{2,1,0:T(2,128)S(1)} collective-permute-done((f32[8,2,640]{2,1,0:T(2,128)S(1)}, f32[8,2,640]{2,1,0:T(2,128)S(1)}, u32[]{:S(2)}, u32[]{:S(2)}) %collective-permute-start.3) | collective-permute-done | bytes 40992 | tf_op jit(solution)/shard_map/ppermute | solution.py:451
  14.4 4.2 %step.1 = (f32[32,128]{1,0:T(8,128)}, f32[16,128]{1,0:T(8,128)}) custom-call(f32[8,2,640]{2,1,0:T(2,128)S(1)} %constant_dynamic-update-slice_fusion.near_ref, f32[8,2,640]{2,1,0:T(2,128)S(1)} %collective-permute-done.3.far_ref, bf16[128,1024]{1,0:T(8,128)(2,1)S(1)} %views.1.near_view, f32[6,128,128]{2,1,0:T(8,128)S(1)} %get-tuple-element.13.rec, ...), custom_call_target="tpu_custom_call" | custom-call | tf_op jit(solution)/shard_map/step/pallas_call | solution.py:502
  (4 shorter events, 0.0 us)
Async XLA Ops:
  1.5 6.9 %copy-start = (s32[16,16]{1,0:T(8,128)S(1)}, s32[16,16]{1,0:T(8,128)}, u32[]{:S(2)}) copy-start(s32[16,16]{1,0:T(8,128)} %occupancy_ref.1) | copy-start | bytes 3076
  1.5 4.9 %collective-permute-start = (f32[1,2,640]{2,1,0:T(2,128)S(1)}, f32[1,2,640]{2,1,0:T(2,128)S(1)}, u32[]{:S(2)}, u32[]{:S(2)}) collective-permute-start(f32[1,2,640]{2,1,0:T(2,128)S(1)} %pack.1), channel_id=1, source_target_pairs={{0,9},{1,8},{2,11},{3,10},{4,13},{5,12},{6,15},{7,14},{8,1},{9,0},... | collective-permute-start | bytes 15368 | tf_op jit(solution)/shard_map/ppermute | solution.py:451
  6.4 2.0 %copy-start.1 = (f32[3,128]{1,0:T(4,128)S(1)}, f32[3,128]{1,0:T(4,128)}, u32[]{:S(2)}) copy-start(f32[3,128]{1,0:T(4,128)} %pos_ref.1) | copy-start | bytes 4612
  6.4 2.0 %copy-start.2 = (f32[3,128]{1,0:T(4,128)S(1)}, f32[3,128]{1,0:T(4,128)}, u32[]{:S(2)}) copy-start(f32[3,128]{1,0:T(4,128)} %nrm_ref.1) | copy-start | bytes 4612
  6.4 2.0 %copy-start.3 = (f32[2,16]{1,0:T(2,128)S(1)}, f32[2,16]{1,0:T(2,128)}, u32[]{:S(2)}) copy-start(f32[2,16]{1,0:T(2,128)} %constant.2.clone.angle_ref) | copy-start | bytes 388
  6.4 2.0 %copy-start.4 = (f32[16]{0:T(128)S(1)}, f32[16]{0:T(128)}, u32[]{:S(2)}) copy-start(f32[16]{0:T(128)} %param.16) | copy-start | bytes 196
  6.4 3.3 %collective-permute-start.1 = (f32[2,2,640]{2,1,0:T(2,128)S(1)}, f32[2,2,640]{2,1,0:T(2,128)S(1)}, u32[]{:S(2)}, u32[]{:S(2)}) collective-permute-start(f32[2,2,640]{2,1,0:T(2,128)S(1)} %pad_maximum_fusion.1), channel_id=1, source_target_pairs={{0,5},{1,4},{2,7},{3,6},{4,1},{5,0},{6,3},{7,2},{8,13},{9,12},{10,... | collective-permute-start | bytes 30728 | tf_op jit(solution)/shard_map/ppermute | solution.py:451
  9.7 3.3 %collective-permute-start.2 = (f32[4,2,640]{2,1,0:T(2,128)S(1)}, f32[4,2,640]{2,1,0:T(2,128)S(1)}, u32[]{:S(2)}, u32[]{:S(2)}) collective-permute-start(f32[4,2,640]{2,1,0:T(2,128)S(1)} %pad_maximum_fusion), channel_id=1, source_target_pairs={{0,3},{1,2},{2,1},{3,0},{4,7},{5,6},{6,5},{7,4},{8,11},{9,10},{10,... | collective-permute-start | bytes 61448 | tf_op jit(solution)/shard_map/ppermute | solution.py:451
  13.0 1.4 %collective-permute-start.3 = (f32[8,2,640]{2,1,0:T(2,128)S(1)}, f32[8,2,640]{2,1,0:T(2,128)S(1)}, u32[]{:S(2)}, u32[]{:S(2)}) collective-permute-start(f32[8,2,640]{2,1,0:T(2,128)S(1)} %constant_dynamic-update-slice_fusion.near_ref), channel_id=1, source_target_pairs={{0,1},{1,0},{2,3},{3,2},{4,5},{5,4},{6,7},{7,6},{8,9},{9,8},{10,11... | collective-permute-start | bytes 122888 | tf_op jit(solution)/shard_map/ppermute | solution.py:451

commit v5 on v4

--- a/solution.py
+++ b/solution.py
@@ -15,7 +15,7 @@
 shade_width = 0.1
 reach_offset = 0.05
 tiny = 1e-30
-table_unit = 28672.0
+table_unit = 28672.0 * 65536.0
 
 PX, PY, PZ, NX, NY, NZ, AREA, ALBEDO, TOP, SAMPLES, ITEMS = range(11)
 halves = 2
@@ -117,15 +117,16 @@
     sel_ref[...] = jnp.broadcast_to(others[:blocks, 4:5], (blocks, width))
 
 
-def put_views(view, first, src, weight, rec):
+def put_views(view, first, src, weight, rec, ties=None):
     width = rec.shape[1]
     scale = src[AREA] * weight * (1.0 / math.pi)
     lanes = pl.ds(first, width)
     for part in range(0, width, 2 * group):
         pieces = []
+        east = src[PX] if ties is None else src[PX] + ties[part // (2 * group)]
         for half in range(2):
             at = pl.ds(part + half * group, group)
-            dx = rec[0, at, :] - src[PX]
+            dx = rec[0, at, :] - east
             dy = rec[1, at, :] - src[PY]
             dz = rec[2, at, :] - src[PZ]
             facing = jnp.maximum(
@@ -243,17 +244,21 @@
         rows = jnp.where(lane >= part, near, far)
         return pltpu.roll(rows, (width - part) % width, 1)
 
+    def unfold(flat):
+        return (flat.astype(f32), (flat << 16).astype(f32))
+
     unit = table_unit if tabled else 1.0
     each = -(-width // blocks)
     if tabled:
         east, north = [
-            jnp.floor(tab[axis] * unit + 0.5).astype(jnp.int32) for axis in (PX, PY)
+            jnp.floor(tab[axis] * (unit / 65536.0) + 0.5).astype(jnp.int32) for axis in (PX, PY)
         ]
-        spot_ref[0] = east.astype(f32)
-        spot_ref[1] = north.astype(f32)
+        flat = (east << 16) | (north & 0xFFFF)
+        spot_ref[0], spot_ref[1] = unfold(flat)
+        spot_ref[0] += 8192.0
         spot_ref[2] = tab[PZ] * unit
         for first in (0, blocks):
-            flat_ring[pl.ds(first, blocks), :] = (east << 16) | (north & 0xFFFF)
+            flat_ring[pl.ds(first, blocks), :] = flat
             ring[pl.ds(first, blocks), :] = spot_ref[2]
         near_flat, far_flat = [flat_ring[pl.ds(first, blocks), :] for first in (0, 1)]
         near_top, far_top = [ring[pl.ds(first, blocks), :] for first in (0, 1)]
@@ -272,32 +277,34 @@
                 line = 2 * blocks * axis + first
                 ring[pl.ds(line, blocks), :] = tab[axis]
 
-    def turn(block):
-        for number in range(each):
-            first = block * each + number
-            amount = (width - 1 - first) % width
-            flat = pltpu.roll(flat_chosen[first], amount, 1)
-            top = pltpu.roll(chosen[first], amount, 1)
-            east = (flat >> 16).astype(f32)
-            north = ((flat << 16) >> 16).astype(f32)
-            for axis, rows in enumerate((east, north, top)):
-                line = pl.multiple_of((first * 3 + axis) * double, group)
-                turned[pl.ds(line, blocks), :] = rows
-                turned[pl.ds(line + blocks, blocks), :] = rows
+    def turn(first):
+        amount = (width - 1 - first) % width
+        flat = pltpu.roll(flat_chosen[first], amount, 1)
+        top = pltpu.roll(chosen[first], amount, 1)
+        east, north = unfold(flat)
+        for axis, rows in enumerate((east, north, top)):
+            line = pl.multiple_of((first * 3 + axis) * double, group)
+            turned[pl.ds(line, blocks), :] = rows
+            turned[pl.ds(line + blocks, blocks), :] = rows
         return jnp.where(east[:group] > 2.0 * table_unit, 1.0, 0.0)
 
-    def view_block(slot, carry):
+    parts = width // (2 * group)
+    turns = -(-each * blocks // (blocks // 2))
+
+    def view_block(slot, ties):
         block = me ^ origin_of(slot + blocks // 2, masks)
         src = [row_of(tab.at[item], block, group) for item in range(7)]
         weight = row_of(sel, block, group)
+        later = list(ties)
         if tabled:
-            src[PX] = src[PX] + carry
-            carry = turn(2 * slot)
-            turn(2 * slot + 1)
-        put_views(view, pl.multiple_of(slot * width, width), src, weight, rec)
-        return carry
-
-    lax.fori_loop(0, blocks // 2, view_block, jnp.zeros((group, width), f32), unroll=4)
+            for number in range(turns):
+                later[number * parts // turns] = turn(slot * turns + number)
+        first = pl.multiple_of(slot * width, width)
+        put_views(view, first, src, weight, rec, ties)
+        return tuple(later)
+
+    start = (jnp.zeros((group, width), f32),) * parts
+    lax.fori_loop(0, blocks // 2, view_block, start, unroll=2)
 
     lookup.wait()
 
@@ -320,7 +327,9 @@
                         there.append(turn_rows(part, near, far))
                 dx = there[0] - here[0]
                 dy = there[1] - here[1]
-                square = jnp.maximum(dx * dx + dy * dy, tiny * unit * unit)
+                square = dx * dx + dy * dy
+                if not tabled:
+                    square = jnp.maximum(square, tiny)
                 reach = square * lax.rsqrt(square) + reach_offset * unit
                 return jnp.maximum(best, (there[2] - here[2]) / reach)
 

time: 18.8 us -> 18.6 us (0.989)
  no operation moved by 1% of the time
where the time goes in v5:
time: 18.6 us; the launch traced here: 18.5 us
  starting transfers between devices  7.71 us (41%)
  Pallas kernels  5.7 us (31%)
  waiting for transfers between devices  4.29 us (23%)
  between operations  0.69 us (4%)
    ppermute x4, starting transfers between devices, body(): lax.ppermute(near, axes, [(index, index ^ mask) for index in range(blocks)])  7.71 us
    ppermute x4, waiting for transfers between devices, body(): lax.ppermute(near, axes, [(index, index ^ mask) for index in range(blocks)])  4.29 us
    pallas_call x1, Pallas kernels, body(): call(near, far, near_view, rec, sun, sel, *map(in_hbm, (albedo[None], con...  4.07 us
    pallas_call x1, Pallas kernels, body(): pack(*map(in_hbm, (positions, normals, area[None], albedo[None], soil, sa...  0.81 us
    pallas_call x1, Pallas kernels, body(): near_view = look(near, rec, sel)  0.52 us
  transfers between devices with their start and end apart: 4, of which 4 were waited for; matrix products, arithmetic and copies ran while one was open for 0% of the time, Pallas kernels for 4%

profile of v5, /device:TPU:0, one launch (start us, length us, event | category | flops | bytes accessed | tf_op | source)
XLA Modules:
  0.0 18.5 jit_solution(2943103417387724906)
XLA Ops:
  0.6 0.8 %pack.1 = f32[1,2,640]{2,1,0:T(2,128)S(1)} custom-call(f32[3,128]{1,0:T(4,128)} %pos_ref.1, f32[3,128]{1,0:T(4,128)} %nrm_ref.1, f32[1,128]{1,0:T(1,128)} %bitcast.8, f32[1,128]{1,0:T(1,128)} %bitcast.5, f32[32,128]{1,0:T(8,128)} %soil_hbm.3, s32[1,32]{1,0:T(1,128)} %samples_hbm.1), custom_call_target="tpu_custom_call" | custom-call | tf_op jit(solution)/shard_map/pack/pallas_call | solution.py:431
  1.5 0.0 copy-start
  1.5 3.6 %collective-permute-start = (f32[1,2,640]{2,1,0:T(2,128)S(1)}, f32[1,2,640]{2,1,0:T(2,128)S(1)}, u32[]{:S(2)}, u32[]{:S(2)}) collective-permute-start(f32[1,2,640]{2,1,0:T(2,128)S(1)} %pack.1), channel_id=1, source_target_pairs={{0,9},{1,8},{2,11},{3,10},{4,13},{5,12},{6,15},{7,14},{8,1},{9,0},... | collective-permute-start | bytes 15368 | tf_op jit(solution)/shard_map/ppermute | solution.py:460
  5.0 1.3 %collective-permute-done = f32[1,2,640]{2,1,0:T(2,128)S(1)} collective-permute-done((f32[1,2,640]{2,1,0:T(2,128)S(1)}, f32[1,2,640]{2,1,0:T(2,128)S(1)}, u32[]{:S(2)}, u32[]{:S(2)}) %collective-permute-start) | collective-permute-done | bytes 5152 | tf_op jit(solution)/shard_map/ppermute | solution.py:460
  6.4 0.0 copy-start.1
  6.4 0.0 copy-start.2
  6.4 0.0 copy-start.3
  6.4 0.0 copy-start.4
  6.4 1.9 %collective-permute-start.1 = (f32[2,2,640]{2,1,0:T(2,128)S(1)}, f32[2,2,640]{2,1,0:T(2,128)S(1)}, u32[]{:S(2)}, u32[]{:S(2)}) collective-permute-start(f32[2,2,640]{2,1,0:T(2,128)S(1)} %pad_maximum_fusion.1), channel_id=1, source_target_pairs={{0,5},{1,4},{2,7},{3,6},{4,1},{5,0},{6,3},{7,2},{8,13},{9,12},{10,... | collective-permute-start | bytes 30728 | tf_op jit(solution)/shard_map/ppermute | solution.py:460
  8.3 0.0 copy-done
  8.4 0.0 copy-done.1
  8.4 0.0 copy-done.2
  8.4 0.0 copy-done.3
  8.4 0.0 copy-done.4
  8.4 0.3 %prepare.1 = (f32[6,128,128]{2,1,0:T(8,128)S(1)}, f32[4,16,128]{2,1,0:T(8,128)S(1)}, f32[16,128]{1,0:T(8,128)S(1)}) custom-call(f32[3,128]{1,0:T(4,128)S(1)} %copy-done.1, f32[3,128]{1,0:T(4,128)S(1)} %copy-done.2, f32[2,16]{1,0:T(2,128)S(1)} %copy-done.3, f32[1,16]{1,0:T(1,128)S(1)} %bitcast.4, s32[16,16]{1,0:T(8,128)S(1)} %copy-done), custom_call_target="tpu_custom_call" | custom-call | tf_op jit(solution)/shard_map/prepare/pallas_call | solution.py:450
  8.7 1.1 %collective-permute-done.1 = f32[2,2,640]{2,1,0:T(2,128)S(1)} collective-permute-done((f32[2,2,640]{2,1,0:T(2,128)S(1)}, f32[2,2,640]{2,1,0:T(2,128)S(1)}, u32[]{:S(2)}, u32[]{:S(2)}) %collective-permute-start.1) | collective-permute-done | bytes 10272 | tf_op jit(solution)/shard_map/ppermute | solution.py:460
  9.7 1.7 %collective-permute-start.2 = (f32[4,2,640]{2,1,0:T(2,128)S(1)}, f32[4,2,640]{2,1,0:T(2,128)S(1)}, u32[]{:S(2)}, u32[]{:S(2)}) collective-permute-start(f32[4,2,640]{2,1,0:T(2,128)S(1)} %pad_maximum_fusion), channel_id=1, source_target_pairs={{0,3},{1,2},{2,1},{3,0},{4,7},{5,6},{6,5},{7,4},{8,11},{9,10},{10,... | collective-permute-start | bytes 61448 | tf_op jit(solution)/shard_map/ppermute | solution.py:460
  11.5 1.5 %collective-permute-done.2 = f32[4,2,640]{2,1,0:T(2,128)S(1)} collective-permute-done((f32[4,2,640]{2,1,0:T(2,128)S(1)}, f32[4,2,640]{2,1,0:T(2,128)S(1)}, u32[]{:S(2)}, u32[]{:S(2)}) %collective-permute-start.2) | collective-permute-done | bytes 20512 | tf_op jit(solution)/shard_map/ppermute | solution.py:460
  13.0 0.5 %collective-permute-start.3 = (f32[8,2,640]{2,1,0:T(2,128)S(1)}, f32[8,2,640]{2,1,0:T(2,128)S(1)}, u32[]{:S(2)}, u32[]{:S(2)}) collective-permute-start(f32[8,2,640]{2,1,0:T(2,128)S(1)} %constant_dynamic-update-slice_fusion.near_ref), channel_id=1, source_target_pairs={{0,1},{1,0},{2,3},{3,2},{4,5},{5,4},{6,7},{7,6},{8,9},{9,8},{10,11... | collective-permute-start | bytes 122888 | tf_op jit(solution)/shard_map/ppermute | solution.py:460
  13.5 0.5 %views.1.near_view = bf16[128,1024]{1,0:T(8,128)(2,1)S(1)} custom-call(f32[8,2,640]{2,1,0:T(2,128)S(1)} %constant_dynamic-update-slice_fusion.near_ref, f32[6,128,128]{2,1,0:T(8,128)S(1)} %get-tuple-element.13.rec, f32[16,128]{1,0:T(8,128)S(1)} %get-tuple-element.14.sel), custom_call_target="tpu_custom_call" | custom-call | tf_op jit(solution)/shard_map/views/pallas_call | solution.py:470
  14.0 0.4 %collective-permute-done.3.far_ref = f32[8,2,640]{2,1,0:T(2,128)S(1)} collective-permute-done((f32[8,2,640]{2,1,0:T(2,128)S(1)}, f32[8,2,640]{2,1,0:T(2,128)S(1)}, u32[]{:S(2)}, u32[]{:S(2)}) %collective-permute-start.3) | collective-permute-done | bytes 40992 | tf_op jit(solution)/shard_map/ppermute | solution.py:460
  14.4 4.1 %step.1 = (f32[32,128]{1,0:T(8,128)}, f32[16,128]{1,0:T(8,128)}) custom-call(f32[8,2,640]{2,1,0:T(2,128)S(1)} %constant_dynamic-update-slice_fusion.near_ref, f32[8,2,640]{2,1,0:T(2,128)S(1)} %collective-permute-done.3.far_ref, bf16[128,1024]{1,0:T(8,128)(2,1)S(1)} %views.1.near_view, f32[6,128,128]{2,1,0:T(8,128)S(1)} %get-tuple-element.13.rec, ...), custom_call_target="tpu_custom_call" | custom-call | tf_op jit(solution)/shard_map/step/pallas_call | solution.py:511
  (4 shorter events, 0.0 us)
Async XLA Ops:
  1.5 6.9 %copy-start = (s32[16,16]{1,0:T(8,128)S(1)}, s32[16,16]{1,0:T(8,128)}, u32[]{:S(2)}) copy-start(s32[16,16]{1,0:T(8,128)} %occupancy_ref.1) | copy-start | bytes 3076
  1.5 4.9 %collective-permute-start = (f32[1,2,640]{2,1,0:T(2,128)S(1)}, f32[1,2,640]{2,1,0:T(2,128)S(1)}, u32[]{:S(2)}, u32[]{:S(2)}) collective-permute-start(f32[1,2,640]{2,1,0:T(2,128)S(1)} %pack.1), channel_id=1, source_target_pairs={{0,9},{1,8},{2,11},{3,10},{4,13},{5,12},{6,15},{7,14},{8,1},{9,0},... | collective-permute-start | bytes 15368 | tf_op jit(solution)/shard_map/ppermute | solution.py:460
  6.4 2.0 %copy-start.1 = (f32[3,128]{1,0:T(4,128)S(1)}, f32[3,128]{1,0:T(4,128)}, u32[]{:S(2)}) copy-start(f32[3,128]{1,0:T(4,128)} %pos_ref.1) | copy-start | bytes 4612
  6.4 2.0 %copy-start.2 = (f32[3,128]{1,0:T(4,128)S(1)}, f32[3,128]{1,0:T(4,128)}, u32[]{:S(2)}) copy-start(f32[3,128]{1,0:T(4,128)} %nrm_ref.1) | copy-start | bytes 4612
  6.4 2.0 %copy-start.3 = (f32[2,16]{1,0:T(2,128)S(1)}, f32[2,16]{1,0:T(2,128)}, u32[]{:S(2)}) copy-start(f32[2,16]{1,0:T(2,128)} %constant.2.clone.angle_ref) | copy-start | bytes 388
  6.4 2.0 %copy-start.4 = (f32[16]{0:T(128)S(1)}, f32[16]{0:T(128)}, u32[]{:S(2)}) copy-start(f32[16]{0:T(128)} %param.16) | copy-start | bytes 196
  6.4 3.3 %collective-permute-start.1 = (f32[2,2,640]{2,1,0:T(2,128)S(1)}, f32[2,2,640]{2,1,0:T(2,128)S(1)}, u32[]{:S(2)}, u32[]{:S(2)}) collective-permute-start(f32[2,2,640]{2,1,0:T(2,128)S(1)} %pad_maximum_fusion.1), channel_id=1, source_target_pairs={{0,5},{1,4},{2,7},{3,6},{4,1},{5,0},{6,3},{7,2},{8,13},{9,12},{10,... | collective-permute-start | bytes 30728 | tf_op jit(solution)/shard_map/ppermute | solution.py:460
  9.7 3.3 %collective-permute-start.2 = (f32[4,2,640]{2,1,0:T(2,128)S(1)}, f32[4,2,640]{2,1,0:T(2,128)S(1)}, u32[]{:S(2)}, u32[]{:S(2)}) collective-permute-start(f32[4,2,640]{2,1,0:T(2,128)S(1)} %pad_maximum_fusion), channel_id=1, source_target_pairs={{0,3},{1,2},{2,1},{3,0},{4,7},{5,6},{6,5},{7,4},{8,11},{9,10},{10,... | collective-permute-start | bytes 61448 | tf_op jit(solution)/shard_map/ppermute | solution.py:460
  13.0 1.4 %collective-permute-start.3 = (f32[8,2,640]{2,1,0:T(2,128)S(1)}, f32[8,2,640]{2,1,0:T(2,128)S(1)}, u32[]{:S(2)}, u32[]{:S(2)}) collective-permute-start(f32[8,2,640]{2,1,0:T(2,128)S(1)} %constant_dynamic-update-slice_fusion.near_ref), channel_id=1, source_target_pairs={{0,1},{1,0},{2,3},{3,2},{4,5},{5,4},{6,7},{7,6},{8,9},{9,8},{10,11... | collective-permute-start | bytes 122888 | tf_op jit(solution)/shard_map/ppermute | solution.py:460

commit v6 on v5

--- a/solution.py
+++ b/solution.py
@@ -183,8 +183,6 @@
     ring,
     flat_ring,
     turned,
-    chosen,
-    flat_chosen,
     view,
     lit,
     glow,
@@ -260,16 +258,6 @@
         for first in (0, blocks):
             flat_ring[pl.ds(first, blocks), :] = flat
             ring[pl.ds(first, blocks), :] = spot_ref[2]
-        near_flat, far_flat = [flat_ring[pl.ds(first, blocks), :] for first in (0, 1)]
-        near_top, far_top = [ring[pl.ds(first, blocks), :] for first in (0, 1)]
-
-        def choose(number, carry):
-            keep = lane > number
-            flat_chosen[number] = jnp.where(keep, near_flat, far_flat)
-            chosen[number] = jnp.where(keep, near_top, far_top)
-            return carry
-
-        lax.fori_loop(0, each * blocks, choose, 0, unroll=16)
     else:
         for axis in range(3):
             spot_ref[axis] = tab[axis]
@@ -279,8 +267,13 @@
 
     def turn(first):
         amount = (width - 1 - first) % width
-        flat = pltpu.roll(flat_chosen[first], amount, 1)
-        top = pltpu.roll(chosen[first], amount, 1)
+        keep = lane > first
+        flat, top = [
+            jnp.where(keep, ref[pl.ds(0, blocks), :], ref[pl.ds(1, blocks), :])
+            for ref in (flat_ring, ring)
+        ]
+        flat = pltpu.roll(flat, amount, 1)
+        top = pltpu.roll(top, amount, 1)
         east, north = unfold(flat)
         for axis, rows in enumerate((east, north, top)):
             line = pl.multiple_of((first * 3 + axis) * double, group)
@@ -478,8 +471,6 @@
         ((2 * blocks * (1 if tabled else 3), width), f32),
         ((2 * blocks, width), i32),
         ((turned if tabled else group, width), f32),
-        ((each * blocks, blocks, width) if tabled else (group, width), f32),
-        ((each * blocks, blocks, width) if tabled else (group, width), i32),
         ((width, blocks // 2 * width), jnp.bfloat16),
         ((epochs * blocks, width), f32),
         ((epochs * blocks, width), f32),

time: 18.6 us -> 18.6 us (level)
  no operation moved by 1% of the time
where the time goes in v6:
time: 18.6 us; the launch traced here: 18.4 us
  starting transfers between devices  7.71 us (41%)
  Pallas kernels  5.64 us (30%)
  waiting for transfers between devices  4.29 us (23%)
  between operations  0.69 us (4%)
    ppermute x4, starting transfers between devices, body(): lax.ppermute(near, axes, [(index, index ^ mask) for index in range(blocks)])  7.71 us
    ppermute x4, waiting for transfers between devices, body(): lax.ppermute(near, axes, [(index, index ^ mask) for index in range(blocks)])  4.29 us
    pallas_call x1, Pallas kernels, body(): call(near, far, near_view, rec, sun, sel, *map(in_hbm, (albedo[None], con...  4 us
    pallas_call x1, Pallas kernels, body(): pack(*map(in_hbm, (positions, normals, area[None], albedo[None], soil, sa...  0.81 us
    pallas_call x1, Pallas kernels, body(): near_view = look(near, rec, sel)  0.52 us
  transfers between devices with their start and end apart: 4, of which 4 were waited for; matrix products, arithmetic and copies ran while one was open for 0% of the time, Pallas kernels for 4%

profile of v6, /device:TPU:0, one launch (start us, length us, event | category | flops | bytes accessed | tf_op | source)
XLA Modules:
  0.0 18.4 jit_solution(6348029886279631221)
XLA Ops:
  0.6 0.8 %pack.1 = f32[1,2,640]{2,1,0:T(2,128)S(1)} custom-call(f32[3,128]{1,0:T(4,128)} %pos_ref.1, f32[3,128]{1,0:T(4,128)} %nrm_ref.1, f32[1,128]{1,0:T(1,128)} %bitcast.8, f32[1,128]{1,0:T(1,128)} %bitcast.5, f32[32,128]{1,0:T(8,128)} %soil_hbm.3, s32[1,32]{1,0:T(1,128)} %samples_hbm.1), custom_call_target="tpu_custom_call" | custom-call | tf_op jit(solution)/shard_map/pack/pallas_call | solution.py:424
  1.5 0.0 copy-start
  1.5 3.6 %collective-permute-start = (f32[1,2,640]{2,1,0:T(2,128)S(1)}, f32[1,2,640]{2,1,0:T(2,128)S(1)}, u32[]{:S(2)}, u32[]{:S(2)}) collective-permute-start(f32[1,2,640]{2,1,0:T(2,128)S(1)} %pack.1), channel_id=1, source_target_pairs={{0,9},{1,8},{2,11},{3,10},{4,13},{5,12},{6,15},{7,14},{8,1},{9,0},... | collective-permute-start | bytes 15368 | tf_op jit(solution)/shard_map/ppermute | solution.py:453
  5.0 1.3 %collective-permute-done = f32[1,2,640]{2,1,0:T(2,128)S(1)} collective-permute-done((f32[1,2,640]{2,1,0:T(2,128)S(1)}, f32[1,2,640]{2,1,0:T(2,128)S(1)}, u32[]{:S(2)}, u32[]{:S(2)}) %collective-permute-start) | collective-permute-done | bytes 5152 | tf_op jit(solution)/shard_map/ppermute | solution.py:453
  6.4 0.0 copy-start.1
  6.4 0.0 copy-start.2
  6.4 0.0 copy-start.3
  6.4 0.0 copy-start.4
  6.4 1.9 %collective-permute-start.1 = (f32[2,2,640]{2,1,0:T(2,128)S(1)}, f32[2,2,640]{2,1,0:T(2,128)S(1)}, u32[]{:S(2)}, u32[]{:S(2)}) collective-permute-start(f32[2,2,640]{2,1,0:T(2,128)S(1)} %pad_maximum_fusion.1), channel_id=1, source_target_pairs={{0,5},{1,4},{2,7},{3,6},{4,1},{5,0},{6,3},{7,2},{8,13},{9,12},{10,... | collective-permute-start | bytes 30728 | tf_op jit(solution)/shard_map/ppermute | solution.py:453
  8.3 0.0 copy-done
  8.4 0.0 copy-done.1
  8.4 0.0 copy-done.2
  8.4 0.0 copy-done.3
  8.4 0.0 copy-done.4
  8.4 0.3 %prepare.1 = (f32[6,128,128]{2,1,0:T(8,128)S(1)}, f32[4,16,128]{2,1,0:T(8,128)S(1)}, f32[16,128]{1,0:T(8,128)S(1)}) custom-call(f32[3,128]{1,0:T(4,128)S(1)} %copy-done.1, f32[3,128]{1,0:T(4,128)S(1)} %copy-done.2, f32[2,16]{1,0:T(2,128)S(1)} %copy-done.3, f32[1,16]{1,0:T(1,128)S(1)} %bitcast.4, s32[16,16]{1,0:T(8,128)S(1)} %copy-done), custom_call_target="tpu_custom_call" | custom-call | tf_op jit(solution)/shard_map/prepare/pallas_call | solution.py:443
  8.7 1.1 %collective-permute-done.1 = f32[2,2,640]{2,1,0:T(2,128)S(1)} collective-permute-done((f32[2,2,640]{2,1,0:T(2,128)S(1)}, f32[2,2,640]{2,1,0:T(2,128)S(1)}, u32[]{:S(2)}, u32[]{:S(2)}) %collective-permute-start.1) | collective-permute-done | bytes 10272 | tf_op jit(solution)/shard_map/ppermute | solution.py:453
  9.7 1.7 %collective-permute-start.2 = (f32[4,2,640]{2,1,0:T(2,128)S(1)}, f32[4,2,640]{2,1,0:T(2,128)S(1)}, u32[]{:S(2)}, u32[]{:S(2)}) collective-permute-start(f32[4,2,640]{2,1,0:T(2,128)S(1)} %pad_maximum_fusion), channel_id=1, source_target_pairs={{0,3},{1,2},{2,1},{3,0},{4,7},{5,6},{6,5},{7,4},{8,11},{9,10},{10,... | collective-permute-start | bytes 61448 | tf_op jit(solution)/shard_map/ppermute | solution.py:453
  11.5 1.5 %collective-permute-done.2 = f32[4,2,640]{2,1,0:T(2,128)S(1)} collective-permute-done((f32[4,2,640]{2,1,0:T(2,128)S(1)}, f32[4,2,640]{2,1,0:T(2,128)S(1)}, u32[]{:S(2)}, u32[]{:S(2)}) %collective-permute-start.2) | collective-permute-done | bytes 20512 | tf_op jit(solution)/shard_map/ppermute | solution.py:453
  13.0 0.5 %collective-permute-start.3 = (f32[8,2,640]{2,1,0:T(2,128)S(1)}, f32[8,2,640]{2,1,0:T(2,128)S(1)}, u32[]{:S(2)}, u32[]{:S(2)}) collective-permute-start(f32[8,2,640]{2,1,0:T(2,128)S(1)} %constant_dynamic-update-slice_fusion.near_ref), channel_id=1, source_target_pairs={{0,1},{1,0},{2,3},{3,2},{4,5},{5,4},{6,7},{7,6},{8,9},{9,8},{10,11... | collective-permute-start | bytes 122888 | tf_op jit(solution)/shard_map/ppermute | solution.py:453
  13.5 0.5 %views.1.near_view = bf16[128,1024]{1,0:T(8,128)(2,1)S(1)} custom-call(f32[8,2,640]{2,1,0:T(2,128)S(1)} %constant_dynamic-update-slice_fusion.near_ref, f32[6,128,128]{2,1,0:T(8,128)S(1)} %get-tuple-element.13.rec, f32[16,128]{1,0:T(8,128)S(1)} %get-tuple-element.14.sel), custom_call_target="tpu_custom_call" | custom-call | tf_op jit(solution)/shard_map/views/pallas_call | solution.py:463
  14.0 0.4 %collective-permute-done.3.far_ref = f32[8,2,640]{2,1,0:T(2,128)S(1)} collective-permute-done((f32[8,2,640]{2,1,0:T(2,128)S(1)}, f32[8,2,640]{2,1,0:T(2,128)S(1)}, u32[]{:S(2)}, u32[]{:S(2)}) %collective-permute-start.3) | collective-permute-done | bytes 40992 | tf_op jit(solution)/shard_map/ppermute | solution.py:453
  14.4 4.0 %step.1 = (f32[32,128]{1,0:T(8,128)}, f32[16,128]{1,0:T(8,128)}) custom-call(f32[8,2,640]{2,1,0:T(2,128)S(1)} %constant_dynamic-update-slice_fusion.near_ref, f32[8,2,640]{2,1,0:T(2,128)S(1)} %collective-permute-done.3.far_ref, bf16[128,1024]{1,0:T(8,128)(2,1)S(1)} %views.1.near_view, f32[6,128,128]{2,1,0:T(8,128)S(1)} %get-tuple-element.13.rec, ...), custom_call_target="tpu_custom_call" | custom-call | tf_op jit(solution)/shard_map/step/pallas_call | solution.py:502
  (4 shorter events, 0.0 us)
Async XLA Ops:
  1.5 6.9 %copy-start = (s32[16,16]{1,0:T(8,128)S(1)}, s32[16,16]{1,0:T(8,128)}, u32[]{:S(2)}) copy-start(s32[16,16]{1,0:T(8,128)} %occupancy_ref.1) | copy-start | bytes 3076
  1.5 4.9 %collective-permute-start = (f32[1,2,640]{2,1,0:T(2,128)S(1)}, f32[1,2,640]{2,1,0:T(2,128)S(1)}, u32[]{:S(2)}, u32[]{:S(2)}) collective-permute-start(f32[1,2,640]{2,1,0:T(2,128)S(1)} %pack.1), channel_id=1, source_target_pairs={{0,9},{1,8},{2,11},{3,10},{4,13},{5,12},{6,15},{7,14},{8,1},{9,0},... | collective-permute-start | bytes 15368 | tf_op jit(solution)/shard_map/ppermute | solution.py:453
  6.4 2.0 %copy-start.1 = (f32[3,128]{1,0:T(4,128)S(1)}, f32[3,128]{1,0:T(4,128)}, u32[]{:S(2)}) copy-start(f32[3,128]{1,0:T(4,128)} %pos_ref.1) | copy-start | bytes 4612
  6.4 2.0 %copy-start.2 = (f32[3,128]{1,0:T(4,128)S(1)}, f32[3,128]{1,0:T(4,128)}, u32[]{:S(2)}) copy-start(f32[3,128]{1,0:T(4,128)} %nrm_ref.1) | copy-start | bytes 4612
  6.4 2.0 %copy-start.3 = (f32[2,16]{1,0:T(2,128)S(1)}, f32[2,16]{1,0:T(2,128)}, u32[]{:S(2)}) copy-start(f32[2,16]{1,0:T(2,128)} %constant.2.clone.angle_ref) | copy-start | bytes 388
  6.4 2.0 %copy-start.4 = (f32[16]{0:T(128)S(1)}, f32[16]{0:T(128)}, u32[]{:S(2)}) copy-start(f32[16]{0:T(128)} %param.16) | copy-start | bytes 196
  6.4 3.3 %collective-permute-start.1 = (f32[2,2,640]{2,1,0:T(2,128)S(1)}, f32[2,2,640]{2,1,0:T(2,128)S(1)}, u32[]{:S(2)}, u32[]{:S(2)}) collective-permute-start(f32[2,2,640]{2,1,0:T(2,128)S(1)} %pad_maximum_fusion.1), channel_id=1, source_target_pairs={{0,5},{1,4},{2,7},{3,6},{4,1},{5,0},{6,3},{7,2},{8,13},{9,12},{10,... | collective-permute-start | bytes 30728 | tf_op jit(solution)/shard_map/ppermute | solution.py:453
  9.7 3.3 %collective-permute-start.2 = (f32[4,2,640]{2,1,0:T(2,128)S(1)}, f32[4,2,640]{2,1,0:T(2,128)S(1)}, u32[]{:S(2)}, u32[]{:S(2)}) collective-permute-start(f32[4,2,640]{2,1,0:T(2,128)S(1)} %pad_maximum_fusion), channel_id=1, source_target_pairs={{0,3},{1,2},{2,1},{3,0},{4,7},{5,6},{6,5},{7,4},{8,11},{9,10},{10,... | collective-permute-start | bytes 61448 | tf_op jit(solution)/shard_map/ppermute | solution.py:453
  13.0 1.4 %collective-permute-start.3 = (f32[8,2,640]{2,1,0:T(2,128)S(1)}, f32[8,2,640]{2,1,0:T(2,128)S(1)}, u32[]{:S(2)}, u32[]{:S(2)}) collective-permute-start(f32[8,2,640]{2,1,0:T(2,128)S(1)} %constant_dynamic-update-slice_fusion.near_ref), channel_id=1, source_target_pairs={{0,1},{1,0},{2,3},{3,2},{4,5},{5,4},{6,7},{7,6},{8,9},{9,8},{10,11... | collective-permute-start | bytes 122888 | tf_op jit(solution)/shard_map/ppermute | solution.py:453

commit v7 on v6

--- a/solution.py
+++ b/solution.py
@@ -103,7 +103,7 @@
     stage[0, pl.ds(0, 3), :] = pos_ref[...]
     stage[0, pl.ds(3, 3), :] = -nrm_ref[...]
     tangent = tan_ref[...]
-    level = lax.rsqrt(1.0 + tangent * tangent)
+    level = solar_flux * lax.rsqrt(1.0 + tangent * tangent)
     stage[1, pl.ds(0, 2), pl.ds(0, epochs)] = angle_ref[...] * level
     stage[1, pl.ds(2, 1), pl.ds(0, epochs)] = tangent * level
     stage[1, pl.ds(3, 1), pl.ds(0, epochs)] = tangent
@@ -300,6 +300,7 @@
     lax.fori_loop(0, blocks // 2, view_block, start, unroll=2)
 
     lookup.wait()
+    tab[TOP] = emissivity * fourth(tab[TOP])
 
     def azimuth(index, carry):
         line, spot = index // held, (index % held) * per_azimuth
@@ -333,10 +334,10 @@
             ]
             incidence = towards[0] * nx + towards[1] * ny + towards[2] * nz
             shade = jax.nn.sigmoid((towards[3] - horizon) * (1.0 / shade_width))
-            direct = solar_flux * jnp.maximum(incidence, 0.0) * shade
-            rows = pl.ds(pl.multiple_of(index * blocks + low, group), chunk)
+            direct = jnp.maximum(incidence, 0.0) * shade
+            rows = pl.ds(low * epochs + index, chunk, stride=epochs)
             lit[rows, :] = direct
-            glow[rows, :] = albedo * direct + emissivity * fourth(top)
+            glow[rows, :] = albedo * direct + top
         return carry
 
     lax.fori_loop(0, epochs, azimuth, 0, unroll=8)
@@ -346,7 +347,7 @@
             pieces = []
             for half in range(2):
                 block = me ^ origin_of(first + 2 * pair + half, masks)
-                piece = glow[pl.ds(block, epochs, stride=blocks), :]
+                piece = glow[pl.ds(pl.multiple_of(block * epochs, group), epochs), :]
                 pieces.append(piece.astype(jnp.bfloat16))
             lanes = pl.ds(pl.multiple_of(pair * (2 * width), 2 * width), 2 * width)
             flux = flux + lax.dot_general(
@@ -362,7 +363,7 @@
     bounce_ref[...] = bounce
     for copy in late:
         copy.wait()
-    direct = lit[pl.ds(me, epochs, stride=blocks), :]
+    direct = lit[pl.ds(pl.multiple_of(me * epochs, group), epochs), :]
     load_ref[...] = (surface_gain * (1.0 - albedo_ref[...])) * (direct + bounce)
 
     count = layers // group

time: 18.6 us -> 18.6 us (level)
  no operation moved by 1% of the time
where the time goes in v7:
time: 18.6 us; the launch traced here: 18.4 us
  starting transfers between devices  7.71 us (41%)
  Pallas kernels  5.66 us (30%)
  waiting for transfers between devices  4.29 us (23%)
  between operations  0.69 us (4%)
    ppermute x4, starting transfers between devices, body(): lax.ppermute(near, axes, [(index, index ^ mask) for index in range(blocks)])  7.71 us
    ppermute x4, waiting for transfers between devices, body(): lax.ppermute(near, axes, [(index, index ^ mask) for index in range(blocks)])  4.29 us
    pallas_call x1, Pallas kernels, body(): call(near, far, near_view, rec, sun, sel, *map(in_hbm, (albedo[None], con...  4.02 us
    pallas_call x1, Pallas kernels, body(): pack(*map(in_hbm, (positions, normals, area[None], albedo[None], soil, sa...  0.81 us
    pallas_call x1, Pallas kernels, body(): near_view = look(near, rec, sel)  0.52 us
  transfers between devices with their start and end apart: 4, of which 4 were waited for; matrix products, arithmetic and copies ran while one was open for 0% of the time, Pallas kernels for 4%

profile of v7, /device:TPU:0, one launch (start us, length us, event | category | flops | bytes accessed | tf_op | source)
XLA Modules:
  0.0 18.4 jit_solution(6649375080290131946)
XLA Ops:
  0.6 0.8 %pack.1 = f32[1,2,640]{2,1,0:T(2,128)S(1)} custom-call(f32[3,128]{1,0:T(4,128)} %pos_ref.1, f32[3,128]{1,0:T(4,128)} %nrm_ref.1, f32[1,128]{1,0:T(1,128)} %bitcast.8, f32[1,128]{1,0:T(1,128)} %bitcast.5, f32[32,128]{1,0:T(8,128)} %soil_hbm.3, s32[1,32]{1,0:T(1,128)} %samples_hbm.1), custom_call_target="tpu_custom_call" | custom-call | tf_op jit(solution)/shard_map/pack/pallas_call | solution.py:425
  1.5 0.0 copy-start
  1.5 3.6 %collective-permute-start = (f32[1,2,640]{2,1,0:T(2,128)S(1)}, f32[1,2,640]{2,1,0:T(2,128)S(1)}, u32[]{:S(2)}, u32[]{:S(2)}) collective-permute-start(f32[1,2,640]{2,1,0:T(2,128)S(1)} %pack.1), channel_id=1, source_target_pairs={{0,9},{1,8},{2,11},{3,10},{4,13},{5,12},{6,15},{7,14},{8,1},{9,0},... | collective-permute-start | bytes 15368 | tf_op jit(solution)/shard_map/ppermute | solution.py:454
  5.0 1.3 %collective-permute-done = f32[1,2,640]{2,1,0:T(2,128)S(1)} collective-permute-done((f32[1,2,640]{2,1,0:T(2,128)S(1)}, f32[1,2,640]{2,1,0:T(2,128)S(1)}, u32[]{:S(2)}, u32[]{:S(2)}) %collective-permute-start) | collective-permute-done | bytes 5152 | tf_op jit(solution)/shard_map/ppermute | solution.py:454
  6.4 0.0 copy-start.1
  6.4 0.0 copy-start.2
  6.4 0.0 copy-start.3
  6.4 0.0 copy-start.4
  6.4 1.9 %collective-permute-start.1 = (f32[2,2,640]{2,1,0:T(2,128)S(1)}, f32[2,2,640]{2,1,0:T(2,128)S(1)}, u32[]{:S(2)}, u32[]{:S(2)}) collective-permute-start(f32[2,2,640]{2,1,0:T(2,128)S(1)} %pad_maximum_fusion.1), channel_id=1, source_target_pairs={{0,5},{1,4},{2,7},{3,6},{4,1},{5,0},{6,3},{7,2},{8,13},{9,12},{10,... | collective-permute-start | bytes 30728 | tf_op jit(solution)/shard_map/ppermute | solution.py:454
  8.3 0.0 copy-done
  8.4 0.0 copy-done.1
  8.4 0.0 copy-done.2
  8.4 0.0 copy-done.3
  8.4 0.0 copy-done.4
  8.4 0.3 %prepare.1 = (f32[6,128,128]{2,1,0:T(8,128)S(1)}, f32[4,16,128]{2,1,0:T(8,128)S(1)}, f32[16,128]{1,0:T(8,128)S(1)}) custom-call(f32[3,128]{1,0:T(4,128)S(1)} %copy-done.1, f32[3,128]{1,0:T(4,128)S(1)} %copy-done.2, f32[2,16]{1,0:T(2,128)S(1)} %copy-done.3, f32[1,16]{1,0:T(1,128)S(1)} %bitcast.4, s32[16,16]{1,0:T(8,128)S(1)} %copy-done), custom_call_target="tpu_custom_call" | custom-call | tf_op jit(solution)/shard_map/prepare/pallas_call | solution.py:444
  8.7 1.1 %collective-permute-done.1 = f32[2,2,640]{2,1,0:T(2,128)S(1)} collective-permute-done((f32[2,2,640]{2,1,0:T(2,128)S(1)}, f32[2,2,640]{2,1,0:T(2,128)S(1)}, u32[]{:S(2)}, u32[]{:S(2)}) %collective-permute-start.1) | collective-permute-done | bytes 10272 | tf_op jit(solution)/shard_map/ppermute | solution.py:454
  9.7 1.7 %collective-permute-start.2 = (f32[4,2,640]{2,1,0:T(2,128)S(1)}, f32[4,2,640]{2,1,0:T(2,128)S(1)}, u32[]{:S(2)}, u32[]{:S(2)}) collective-permute-start(f32[4,2,640]{2,1,0:T(2,128)S(1)} %pad_maximum_fusion), channel_id=1, source_target_pairs={{0,3},{1,2},{2,1},{3,0},{4,7},{5,6},{6,5},{7,4},{8,11},{9,10},{10,... | collective-permute-start | bytes 61448 | tf_op jit(solution)/shard_map/ppermute | solution.py:454
  11.5 1.5 %collective-permute-done.2 = f32[4,2,640]{2,1,0:T(2,128)S(1)} collective-permute-done((f32[4,2,640]{2,1,0:T(2,128)S(1)}, f32[4,2,640]{2,1,0:T(2,128)S(1)}, u32[]{:S(2)}, u32[]{:S(2)}) %collective-permute-start.2) | collective-permute-done | bytes 20512 | tf_op jit(solution)/shard_map/ppermute | solution.py:454
  13.0 0.5 %collective-permute-start.3 = (f32[8,2,640]{2,1,0:T(2,128)S(1)}, f32[8,2,640]{2,1,0:T(2,128)S(1)}, u32[]{:S(2)}, u32[]{:S(2)}) collective-permute-start(f32[8,2,640]{2,1,0:T(2,128)S(1)} %constant_dynamic-update-slice_fusion.near_ref), channel_id=1, source_target_pairs={{0,1},{1,0},{2,3},{3,2},{4,5},{5,4},{6,7},{7,6},{8,9},{9,8},{10,11... | collective-permute-start | bytes 122888 | tf_op jit(solution)/shard_map/ppermute | solution.py:454
  13.5 0.5 %views.1.near_view = bf16[128,1024]{1,0:T(8,128)(2,1)S(1)} custom-call(f32[8,2,640]{2,1,0:T(2,128)S(1)} %constant_dynamic-update-slice_fusion.near_ref, f32[6,128,128]{2,1,0:T(8,128)S(1)} %get-tuple-element.13.rec, f32[16,128]{1,0:T(8,128)S(1)} %get-tuple-element.14.sel), custom_call_target="tpu_custom_call" | custom-call | tf_op jit(solution)/shard_map/views/pallas_call | solution.py:464
  14.0 0.4 %collective-permute-done.3.far_ref = f32[8,2,640]{2,1,0:T(2,128)S(1)} collective-permute-done((f32[8,2,640]{2,1,0:T(2,128)S(1)}, f32[8,2,640]{2,1,0:T(2,128)S(1)}, u32[]{:S(2)}, u32[]{:S(2)}) %collective-permute-start.3) | collective-permute-done | bytes 40992 | tf_op jit(solution)/shard_map/ppermute | solution.py:454
  14.4 4.0 %step.1 = (f32[32,128]{1,0:T(8,128)}, f32[16,128]{1,0:T(8,128)}) custom-call(f32[8,2,640]{2,1,0:T(2,128)S(1)} %constant_dynamic-update-slice_fusion.near_ref, f32[8,2,640]{2,1,0:T(2,128)S(1)} %collective-permute-done.3.far_ref, bf16[128,1024]{1,0:T(8,128)(2,1)S(1)} %views.1.near_view, f32[6,128,128]{2,1,0:T(8,128)S(1)} %get-tuple-element.13.rec, ...), custom_call_target="tpu_custom_call" | custom-call | tf_op jit(solution)/shard_map/step/pallas_call | solution.py:503
  (4 shorter events, 0.0 us)
Async XLA Ops:
  1.5 6.9 %copy-start = (s32[16,16]{1,0:T(8,128)S(1)}, s32[16,16]{1,0:T(8,128)}, u32[]{:S(2)}) copy-start(s32[16,16]{1,0:T(8,128)} %occupancy_ref.1) | copy-start | bytes 3076
  1.5 4.9 %collective-permute-start = (f32[1,2,640]{2,1,0:T(2,128)S(1)}, f32[1,2,640]{2,1,0:T(2,128)S(1)}, u32[]{:S(2)}, u32[]{:S(2)}) collective-permute-start(f32[1,2,640]{2,1,0:T(2,128)S(1)} %pack.1), channel_id=1, source_target_pairs={{0,9},{1,8},{2,11},{3,10},{4,13},{5,12},{6,15},{7,14},{8,1},{9,0},... | collective-permute-start | bytes 15368 | tf_op jit(solution)/shard_map/ppermute | solution.py:454
  6.4 2.0 %copy-start.1 = (f32[3,128]{1,0:T(4,128)S(1)}, f32[3,128]{1,0:T(4,128)}, u32[]{:S(2)}) copy-start(f32[3,128]{1,0:T(4,128)} %pos_ref.1) | copy-start | bytes 4612
  6.4 2.0 %copy-start.2 = (f32[3,128]{1,0:T(4,128)S(1)}, f32[3,128]{1,0:T(4,128)}, u32[]{:S(2)}) copy-start(f32[3,128]{1,0:T(4,128)} %nrm_ref.1) | copy-start | bytes 4612
  6.4 2.0 %copy-start.3 = (f32[2,16]{1,0:T(2,128)S(1)}, f32[2,16]{1,0:T(2,128)}, u32[]{:S(2)}) copy-start(f32[2,16]{1,0:T(2,128)} %constant.2.clone.angle_ref) | copy-start | bytes 388
  6.4 2.0 %copy-start.4 = (f32[16]{0:T(128)S(1)}, f32[16]{0:T(128)}, u32[]{:S(2)}) copy-start(f32[16]{0:T(128)} %param.16) | copy-start | bytes 196
  6.4 3.3 %collective-permute-start.1 = (f32[2,2,640]{2,1,0:T(2,128)S(1)}, f32[2,2,640]{2,1,0:T(2,128)S(1)}, u32[]{:S(2)}, u32[]{:S(2)}) collective-permute-start(f32[2,2,640]{2,1,0:T(2,128)S(1)} %pad_maximum_fusion.1), channel_id=1, source_target_pairs={{0,5},{1,4},{2,7},{3,6},{4,1},{5,0},{6,3},{7,2},{8,13},{9,12},{10,... | collective-permute-start | bytes 30728 | tf_op jit(solution)/shard_map/ppermute | solution.py:454
  9.7 3.3 %collective-permute-start.2 = (f32[4,2,640]{2,1,0:T(2,128)S(1)}, f32[4,2,640]{2,1,0:T(2,128)S(1)}, u32[]{:S(2)}, u32[]{:S(2)}) collective-permute-start(f32[4,2,640]{2,1,0:T(2,128)S(1)} %pad_maximum_fusion), channel_id=1, source_target_pairs={{0,3},{1,2},{2,1},{3,0},{4,7},{5,6},{6,5},{7,4},{8,11},{9,10},{10,... | collective-permute-start | bytes 61448 | tf_op jit(solution)/shard_map/ppermute | solution.py:454
  13.0 1.4 %collective-permute-start.3 = (f32[8,2,640]{2,1,0:T(2,128)S(1)}, f32[8,2,640]{2,1,0:T(2,128)S(1)}, u32[]{:S(2)}, u32[]{:S(2)}) collective-permute-start(f32[8,2,640]{2,1,0:T(2,128)S(1)} %constant_dynamic-update-slice_fusion.near_ref), channel_id=1, source_target_pairs={{0,1},{1,0},{2,3},{3,2},{4,5},{5,4},{6,7},{7,6},{8,9},{9,8},{10,11... | collective-permute-start | bytes 122888 | tf_op jit(solution)/shard_map/ppermute | solution.py:454
